TPU v7x, 32 devices: a whole 2x2x4 slice. The times are simulated.
32 devices in a mesh: dp: 2 (over x), ctx: 4 (over y, core), tensor: 4 (over z).
Axes of the slice: x: 2, y: 2, z: 4, core: 2. Of those that a mesh axis runs over, the one named last changes fastest.
Arguments:
- hidden: bfloat16 [2, 16384, 2560], P('dp', 'ctx', 'tensor'), may hold values from -6 to 6
- depth: int32 [2, 16384], P('dp', 'ctx'), may hold values from 1 to 4, as said below
- qkv_weight: bfloat16 [2560, 3, 2560], P(None, None, 'tensor'), may hold values from -0.125 to 0.125
- out_weight: bfloat16 [2560, 2560], P('tensor'), may hold values from -0.125 to 0.125
Outputs:
- update: bfloat16 [2, 16384, 2560], P('dp', 'ctx', 'tensor')
Inputs may be any that keep to these rules, and one draw needn't show every extreme that they name: In every aligned block of 4096 positions of a document at most 1024 tokens have depth at least 3, and some block has exactly 1024; over all documents exactly 4096 tokens do.
All inputs are finite; a program needn't handle non-finite values.
Results may differ from a plain program's by a relative error of at most 0.012.
The roundings to bfloat16 on the way count: a program that leaves them out, or rounds other values in their place, can miss the bound.
Values may be sent and summed in bfloat16 or wider, within the bound.
A program may use at most 256 MiB of HBM per device.

v0:
```python
import jax
import jax.numpy as jnp
from jax import lax
from jax.sharding import PartitionSpec as P

HD = 128
RECURSION = 3
CAP = 1024


score_scale = 0.25
norm_epsilon = 1e-05
head_epsilon = 1e-06


def head_normed(values):
    row_count = values.shape[0]
    per_head = values.reshape(row_count, -1, HD)
    factor = lax.rsqrt(jnp.mean(per_head * per_head, axis=2, keepdims=True) + head_epsilon)
    return (per_head * factor).reshape(row_count, -1).astype(jnp.bfloat16)


def project_rows(token_rows, qkv_weight):
    full_rows = lax.all_gather(token_rows, "tensor", axis=1, tiled=True)
    widened = full_rows.astype(jnp.float32)
    factor = lax.rsqrt(jnp.mean(widened * widened, axis=1, keepdims=True) + norm_epsilon)
    normed = (widened * factor).astype(jnp.bfloat16)
    head_width = qkv_weight.shape[2]
    projection = jnp.dot(
        normed,
        qkv_weight.reshape(qkv_weight.shape[0], 3 * head_width),
        preferred_element_type=jnp.float32,
    )
    queries = head_normed(projection[:, :head_width])
    keys_normed = head_normed(projection[:, head_width : 2 * head_width])
    values_out = projection[:, 2 * head_width :].astype(jnp.bfloat16)
    return jnp.concatenate([queries, keys_normed, values_out], axis=1)


def output_rows(context, out_weight):
    partial_value = jnp.dot(context, out_weight, preferred_element_type=jnp.float32)
    return lax.psum_scatter(
        partial_value.astype(jnp.bfloat16), "tensor", scatter_dimension=1, tiled=True
    )


def per_device(hidden, depth, qkv_weight, out_weight):
    tokens = hidden[0]
    local_len = tokens.shape[0]
    feature_width = tokens.shape[1]
    capacity = CAP
    head_width = out_weight.shape[0]
    heads_here = head_width // HD
    ctx_count = lax.axis_size("ctx")
    ctx_rank = lax.axis_index("ctx")
    active = (depth[0] >= RECURSION).astype(jnp.int32)
    active_count = jnp.sum(active)
    active_rank = jnp.cumsum(active) - 1
    slot_token = (
        jnp.zeros((capacity,), jnp.int32)
        .at[jnp.where(active > 0, active_rank, capacity)]
        .set(jnp.arange(local_len, dtype=jnp.int32), mode="drop")
    )
    filled = jnp.arange(capacity, dtype=jnp.int32) < active_count
    token_rows = jnp.where(filled[:, None], tokens[slot_token], jnp.zeros((), tokens.dtype))
    counts = lax.all_gather(active_count[None], ("dp", "ctx"), axis=0, tiled=True)
    doc_counts = lax.dynamic_slice_in_dim(counts, lax.axis_index("dp") * ctx_count, ctx_count)
    projected = project_rows(token_rows, qkv_weight)
    queries = projected[:, :head_width]
    key_values = projected[:, head_width:]
    query_heads = queries.reshape(capacity, heads_here, HD)
    key_piece = lax.all_gather(key_values, "ctx", axis=0, tiled=True)
    piece_rows = key_piece.shape[0]
    row_index = jnp.arange(piece_rows, dtype=jnp.int32)
    source_shard = row_index // capacity
    source_slot = row_index - source_shard * capacity
    clipped = jnp.clip(source_shard, 0, ctx_count - 1)
    key_filled = (source_shard >= 0) & (source_slot < doc_counts[clipped])
    same_block = (source_shard == ctx_rank)[None, :] & (
        slot_token[source_slot][None, :] <= slot_token[:, None]
    )
    earlier = (source_shard < ctx_rank)[None, :] | same_block
    allowed = earlier & key_filled[None, :] & filled[:, None]
    key_heads = key_piece[:, :head_width].reshape(piece_rows, heads_here, HD)
    value_heads = key_piece[:, head_width:].reshape(piece_rows, heads_here, HD)
    scores = (
        jnp.einsum("qhd,khd->hqk", query_heads, key_heads, preferred_element_type=jnp.float32)
        * score_scale
    )
    weights = jnp.where(allowed[None], jnp.exp(scores), 0.0)
    numerator = jnp.einsum(
        "hqk,khd->qhd",
        weights.astype(jnp.bfloat16),
        value_heads,
        preferred_element_type=jnp.float32,
    )
    denominator = jnp.sum(weights, axis=2)
    numerator, denominator = (numerator, denominator)
    guarded = denominator + (1.0 - filled.astype(jnp.float32))[None, :]
    context = (
        (numerator / jnp.transpose(guarded)[:, :, None])
        .reshape(capacity, head_width)
        .astype(jnp.bfloat16)
    )
    result_rows = output_rows(context, out_weight)
    update = (
        jnp.zeros((local_len, feature_width), jnp.bfloat16)
        .at[jnp.where(filled, slot_token, local_len)]
        .set(result_rows, mode="drop")
    )
    return update[None]


def solution(mesh):
    placed = (P("dp", "ctx", "tensor"), P("dp", "ctx"), P(None, None, "tensor"), P("tensor", None))
    return jax.shard_map(
        per_device, mesh=mesh, in_specs=placed, out_specs=P("dp", "ctx", "tensor"), check_vma=False
    )
```

profile of v0, /device:TPU:0, one launch (start us, length us, event | category | flops | bytes accessed | tf_op | source)
XLA Modules:
  0.0 478.1 jit_solution(8814270308655947177)
XLA Ops:
  11.0 15.5 %scatter_custom_fusion = s32[1024]{0:T(1024)S(1)} fusion(s32[4096]{0:T(1024)S(1)} %bitcast.55, s32[4096]{0:T(1024)S(1)} %iota.35, s32[]{:T(128)} %constant.58.clone.1), kind=kCustom, calls=%fused_computation.67 | custom fusion | bytes 4100 | tf_op jit(solution)/shard_map/scatter | solution.py:62
  27.7 8.4 %gather_fusion = bf16[1024,640]{1,0:T(8,128)(2,1)} fusion(bf16[4096,640]{1,0:T(8,128)(2,1)} %bitcast.40, s32[1024]{0:T(1024)S(1)} %get-tuple-element.11), kind=kCustom, calls=%fused_computation | custom fusion | bytes 2625536 | tf_op jit(solution)/shard_map/gather | solution.py:65
  39.1 14.0 %copy.18 = bf16[2560,3,640]{0,2,1:T(8,128)(2,1)} copy(bf16[2560,3,640]{2,0,1:T(8,128)(2,1)} %param.6) | data formatting | bytes 19660800 | tf_op args[2]
  53.0 86.7 %all-gather.3.cloned.1.call-done = bf16[1024,2560]{1,0:T(8,128)(2,1)} async-done(((bf16[1024,640]{1,0:T(8,128)(2,1)}), bf16[1024,2560]{1,0:T(8,128)(2,1)}) %all-gather.3.cloned.1.call-update) | async-done | bytes 5242896 | tf_op jit(solution)/shard_map/all_gather | solution.py:24
  139.7 3.6 fusion.5
  143.3 15.4 %fusion.7 = f32[1024,1920]{1,0:T(8,128)S(1)} fusion(bf16[2560,1920]{0,1:T(8,128)(2,1)} %bitcast.46, bf16[1024,2560]{1,0:T(8,128)(2,1)} %all-gather.3.cloned.1.call-done, f32[1024]{0:T(1024)S(1)} %add_rsqrt_fusion.2), kind=kOutput, calls=%fused_computation.15 | convolution fusion | flops 10074193920 | bytes 22941696 | tf_op jit(solution)/shard_map/dot_general | solution.py:29
  163.9 3.3 copy.22
  171.0 3.3 copy.23
  174.3 3.2 copy.19
  181.3 3.2 copy.20
  184.5 5.7 %multiply_convert_fusion = (bf16[1024,640]{1,0:T(8,128)(2,1)}, bf16[1024,640]{1,0:T(8,128)(2,1)S(1)}) fusion(f32[1024,640]{1,0:T(8,128)} %copy.23, f32[1024,1920]{1,0:T(8,128)} %copy-done.1, f32[1024,640]{1,0:T(8,128)} %copy.20), kind=kLoop, calls=%fused_computation.21 | loop fusion | flops 2621440 | bytes 13107200 | tf_op jit(solution)/shard_map/convert_element_type | solution.py:20
  194.1 7.9 %all-reduce = s32[8]{0:T(128)S(1)} all-reduce(s32[8]{0:T(128)S(1)} %dynamic-update-slice), channel_id=1, replica_groups=mesh['dp'=2,'ctx'=4,'tensor'=4] {'dp','ctx'}, use_global_device_ids=true, to_apply=%add | all-reduce | flops 8 | bytes 64
  202.1 16.7 %gather_fusion.1 = s32[4096]{0:T(1024)S(1)} fusion(s32[1024]{0:T(1024)S(1)} %scatter_custom_fusion, s32[4096]{0:T(1024)S(1)} %broadcast_clamp_fusion), kind=kCustom, calls=%fused_computation.1 | custom fusion | bytes 49152 | tf_op jit(solution)/shard_map/gather | solution.py:80
  222.7 6.2 %and_and_fusion = pred[1024,4096]{1,0:T(8,128)(4,1)} fusion(s32[4096]{0:T(1024)S(1)} %gather_fusion.1, s32[1024]{0:T(1024)S(1)} %scatter_custom_fusion, pred[1024]{0:T(1024)(128)(4,1)S(1)} %iota_compare_fusion, pred[4096]{0:T(1024)(128)(4,1)S(1)} %fusion.23, pred[4096]{0:T(1024)(128)(4,1)S(1)} %get-tuple-element.19, pred[4096]{0:T(1024)(128)(4,1)S(1)} %get-tuple-element.20), kind=kLoop, calls=%fused_computation.9 | loop fusion | flops 20971520 | bytes 4228096 | tf_op jit(solution)/shard_map/and | solution.py:83
  231.4 29.2 %all-gather.5.cloned.1.call-done = bf16[4096,1280]{1,0:T(8,128)(2,1)} async-done(((bf16[1024,1280]{1,0:T(8,128)(2,1)}), bf16[4096,1280]{1,0:T(8,128)(2,1)}) %all-gather.5.cloned.1.call-update) | async-done | bytes 10485776 | tf_op jit(solution)/shard_map/all_gather | solution.py:72
  260.6 9.0 %fusion.31 = (bf16[4096,640]{1,0:T(8,128)(2,1)}, bf16[4096,640]{1,0:T(8,128)(2,1)}) fusion(bf16[4096,1280]{1,0:T(8,128)(2,1)} %all-gather.5.cloned.1.call-done), kind=kLoop, calls=%fused_computation.72 | loop fusion | bytes 20971520 | tf_op jit(solution)/shard_map/slice | solution.py:84
  269.7 7.9 %copy.21 = bf16[4096,640]{0,1:T(8,128)(2,1)} copy(bf16[4096,640]{1,0:T(8,128)(2,1)} %get-tuple-element.6) | data formatting | bytes 10485760 | tf_op jit(solution)/shard_map/slice | solution.py:85
  277.6 8.0 %copy.25 = bf16[4096,640]{0,1:T(8,128)(2,1)} copy(bf16[4096,640]{1,0:T(8,128)(2,1)} %get-tuple-element.5) | data formatting | bytes 10485760 | tf_op jit(solution)/shard_map/slice | solution.py:84
  285.7 36.3 %fusion = (f32[5,1024]{1,0:T(8,128)S(1)}, f32[5,1024,4096]{2,1,0:T(8,128)}) fusion(pred[1024,4096]{1,0:T(8,128)(4,1)} %and_and_fusion, bf16[1024,5,128]{0,2,1:T(8,128)(2,1)} %bitcast.49, bf16[4096,5,128]{0,2,1:T(8,128)(2,1)} %bitcast.48), kind=kOutput, calls=%fused_computation.5 | convolution fusion | flops 5431618560 | bytes 94654464 | tf_op jit(solution)/shard_map/qhd,khd->hqk/dot_general | solution.py:87
  321.9 30.0 %fusion.10 = bf16[1024,5,128]{0,2,1:T(8,128)(2,1)S(1)} fusion(bf16[4096,5,128]{0,2,1:T(8,128)(2,1)} %bitcast.47, f32[5,1024,4096]{2,1,0:T(8,128)} %get-tuple-element.18, pred[1024,4096]{1,0:T(8,128)(4,1)} %and_and_fusion, f32[1024,5]{0,1:T(8,128)S(1)} %add_bitcast_fusion), kind=kOutput, calls=%fused_computation.20 | convolution fusion | flops 5432934400 | bytes 94654464 | tf_op jit(solution)/shard_map/hqk,khd->qhd/dot_general | solution.py:91
  351.9 6.3 %convolution_convert_fusion = bf16[1024,2560]{1,0:T(8,128)(2,1)} fusion(bf16[1024,640]{0,1:T(8,128)(2,1)S(1)} %bitcast.56, bf16[640,2560]{1,0:T(8,128)(2,1)S(1)} %copy-done), kind=kOutput, calls=%fused_computation.14 | convolution fusion | flops 3358064640 | bytes 9830400 | tf_op jit(solution)/shard_map/dot_general | solution.py:41
  358.3 8.0 %copy.30 = bf16[1024,2560]{0,1:T(8,128)(2,1)} copy(bf16[1024,2560]{1,0:T(8,128)(2,1)} %convolution_convert_fusion) | data formatting | bytes 10485760
  366.2 93.9 %reduce-scatter.4.cloned.1.call-done = bf16[640,1024]{1,0:T(8,128)(2,1)} async-done(((bf16[2560,1024]{1,0:T(8,128)(2,1)}), bf16[640,1024]{1,0:T(8,128)(2,1)}) %reduce-scatter.4.cloned.1.call-update) | async-done | bytes 1310736
  462.6 9.0 %scatter_custom_fusion.1 = bf16[4096,640]{1,0:T(8,128)(2,1)} fusion(s32[1024]{0:T(1024)} %get-tuple-element.12, bf16[1024,640]{1,0:T(8,128)(2,1)} %copy.31, bf16[]{:T(256)} %constant.56.clone.1), kind=kCustom, calls=%fused_computation.23 | custom fusion | bytes 5243392 | tf_op jit(solution)/shard_map/scatter | solution.py:109
  (50 shorter events, 33.9 us)
Async XLA Ops:
  6.5 345.4 %copy-start = (bf16[640,2560]{1,0:T(8,128)(2,1)S(1)}, bf16[640,2560]{1,0:T(8,128)(2,1)}, u32[]{:S(2)}) copy-start(bf16[640,2560]{1,0:T(8,128)(2,1)} %param.7) | copy-start | bytes 9830404
  6.5 133.2 %all-gather.3.cloned.1.call-start = ((), (), s32[]{:S(2)}) async-start(), calls=%async_computation.1 | async-start | bytes 6553600 | tf_op jit(solution)/shard_map/all_gather | solution.py:24
  38.8 221.8 %all-gather.5.cloned.1.call-start = ((), (), s32[]{:S(2)}) async-start(), calls=%async_computation.2 | async-start | bytes 13107200 | tf_op jit(solution)/shard_map/all_gather | solution.py:72
  158.8 5.1 %copy-start.1 = (f32[1024,1920]{1,0:T(8,128)}, f32[1024,1920]{1,0:T(8,128)S(1)}, u32[]{:S(2)}) copy-start(f32[1024,1920]{1,0:T(8,128)S(1)} %fusion.7) | copy-start | bytes 23592964
  184.5 5.7 %copy-start.2 = (bf16[1024,640]{1,0:T(8,128)(2,1)S(1)}, bf16[1024,640]{1,0:T(8,128)(2,1)}, u32[]{:S(2)}) copy-start(bf16[1024,640]{1,0:T(8,128)(2,1)} %slice.52) | copy-start | bytes 3932164
  190.3 1.8 copy-start.3
  192.0 268.2 %reduce-scatter.4.cloned.1.call-start = ((), (), s32[]{:S(2)}) async-start(), calls=%async_computation.3 | async-start | bytes 6553600
Sparse Core Ops, SparseCore 0:
  38.9 100.7 all-gather.2
  192.1 68.4 all-gather.4
  366.4 93.7 reduce-scatter.3
where the time goes:
time: 480 us; the launch traced here: 478 us
  waiting for transfers between devices  210 us (44%)
  local copies, waits for them, and re-layouts  123 us (26%)
  matrix products  88 us (18%)
  other arithmetic  35.6 us (7%)
  between operations  13.3 us (3%)
  blocking collectives  7.93 us (2%)
    unnamed x4, waiting for transfers between devices  94 us
    all_gather x1, waiting for transfers between devices, project_rows(): full_rows = lax.all_gather(token_rows, 'tensor', axis=1, tiled=True)  86.7 us
    dot_general x1, matrix products, per_device(): jnp.einsum('qhd,khd->hqk', query_heads, key_heads, preferred_element_type...  36.3 us
    dot_general x1, matrix products, per_device(): jnp.einsum('hqk,khd->qhd', weights.astype(jnp.bfloat16), value_heads, pre...  30 us
    all_gather x1, waiting for transfers between devices, per_device(): key_piece = lax.all_gather(key_values, 'ctx', axis=0, tiled=True)  29.2 us
    unnamed x14, local copies, waits for them, and re-layouts  27.1 us
    slice x2, local copies, waits for them, and re-layouts, per_device(): key_heads = key_piece[:, :head_width].reshape(piece_rows, heads_here, HD)  17.1 us
    gather x1, local copies, waits for them, and re-layouts, per_device(): slot_token[source_slot][None, :] <= slot_token[:, None]  16.7 us
  transfers between devices with their start and end apart: 3, of which 3 were waited for; matrix products, arithmetic and copies ran while one was open for 9% of the time, Pallas kernels for 0%

commit v1 on v0

v1 whole, which is shorter than its diff:
```python
import functools

import jax
import jax.numpy as jnp
from jax import lax
from jax.experimental import pallas as pl
from jax.experimental.pallas import tpu as pltpu
from jax.sharding import PartitionSpec as P

HD = 128
RECURSION = 3
CAP = 1024
ACT_DEV = 512

score_scale = 0.25
norm_epsilon = 1e-05
head_epsilon = 1e-06
VMEM_LIMIT = 60 * 1024 * 1024
PLANE = ("dp", "ctx")


def project_kernel(x_ref, w_ref, o_ref, normed):
    part = pl.program_id(0)
    shards, rows, width = x_ref.shape

    @pl.when(part == 0)
    def _():
        total = jnp.zeros((rows, 1), jnp.float32)
        for z in range(shards):
            wide = x_ref[z].astype(jnp.float32)
            total = total + jnp.sum(wide * wide, axis=1, keepdims=True)
        factor = lax.rsqrt(total / (shards * width) + norm_epsilon)
        for z in range(shards):
            normed[z] = (x_ref[z].astype(jnp.float32) * factor).astype(jnp.bfloat16)

    acc = jnp.dot(normed[0], w_ref[0, :width], preferred_element_type=jnp.float32)
    for z in range(1, shards):
        acc = acc + jnp.dot(normed[z], w_ref[0, z * width : (z + 1) * width], preferred_element_type=jnp.float32)
    scale = jnp.where(part == 0, score_scale, 1.0)
    for h in range(acc.shape[1] // HD):
        head = acc[:, h * HD : (h + 1) * HD]
        factor = lax.rsqrt(jnp.mean(head * head, axis=1, keepdims=True) + head_epsilon) * scale
        factor = jnp.where(part == 2, 1.0, factor)
        o_ref[0, :, h * HD : (h + 1) * HD] = (head * factor).astype(jnp.bfloat16)


def project(rows_all, weight):
    shards, rows, width = rows_all.shape
    head_width = weight.shape[2]
    return pl.pallas_call(
        project_kernel,
        grid=(3,),
        out_shape=jax.ShapeDtypeStruct((3, rows, head_width), jnp.bfloat16),
        in_specs=[
            pl.BlockSpec((shards, rows, width), lambda p: (0, 0, 0)),
            pl.BlockSpec((1, shards * width, head_width), lambda p: (p, 0, 0)),
        ],
        out_specs=pl.BlockSpec((1, rows, head_width), lambda p: (p, 0, 0)),
        scratch_shapes=[pltpu.VMEM((shards, rows, width), jnp.bfloat16)],
        compiler_params=pltpu.CompilerParams(vmem_limit_bytes=VMEM_LIMIT),
        name="project",
    )(rows_all, weight)


def attend_kernel(docs, meta_ref, q_ref, k_ref, v_ref, o_ref):
    stripe = pl.program_id(1)
    plane, stripes, size, _ = k_ref.shape
    period = plane * size
    me = meta_ref[docs]
    query = q_ref[...]
    q_index = stripe * period + me * size + lax.broadcasted_iota(jnp.int32, (size, 1), 0)
    begin = jnp.zeros((size, 1), jnp.int32)
    for d in range(docs):
        begin = jnp.where(q_index >= meta_ref[d], meta_ref[d], begin)
    lane = lax.broadcasted_iota(jnp.int32, (size, period), 1)

    def tile(at, carry, diagonal):
        num, den = carry
        keys = k_ref[:, pl.ds(at, 1)].reshape(period, HD)
        values = v_ref[:, pl.ds(at, 1)].reshape(period, HD)
        scores = lax.dot_general(query, keys, (((1,), (1,)), ((), ())), preferred_element_type=jnp.float32)
        allowed = lane >= begin - at * period
        if diagonal:
            allowed = allowed & (lane <= q_index - at * period)
        weights = jnp.where(allowed, jnp.exp(scores), 0.0)
        den = den + jnp.sum(weights, axis=1, keepdims=True)
        num = num + jnp.dot(weights.astype(jnp.bfloat16), values, preferred_element_type=jnp.float32)
        return num, den

    carry = (jnp.zeros((size, HD), jnp.float32), jnp.zeros((size, 1), jnp.float32))
    carry = lax.fori_loop(0, stripe, lambda at, c: tile(at, c, False), carry)
    num, den = tile(stripe, carry, True)
    o_ref[...] = (num / den).astype(jnp.bfloat16)


def attend(meta, queries, kv, docs, stripes):
    rows, head_width = queries.shape
    plane = kv.shape[0]
    size = rows // stripes
    heads = head_width // HD
    kv = kv.reshape(plane, 2, stripes, size, head_width)
    return pl.pallas_call(
        functools.partial(attend_kernel, docs),
        grid_spec=pltpu.PrefetchScalarGridSpec(
            num_scalar_prefetch=1,
            grid=(heads, stripes),
            in_specs=[
                pl.BlockSpec((size, HD), lambda h, k, m: (k, h)),
                pl.BlockSpec((plane, None, stripes, size, HD), lambda h, k, m: (0, 0, 0, 0, h)),
                pl.BlockSpec((plane, None, stripes, size, HD), lambda h, k, m: (0, 1, 0, 0, h)),
            ],
            out_specs=pl.BlockSpec((size, HD), lambda h, k, m: (k, h)),
        ),
        out_shape=jax.ShapeDtypeStruct((rows, head_width), jnp.bfloat16),
        compiler_params=pltpu.CompilerParams(vmem_limit_bytes=VMEM_LIMIT),
        name="attend",
    )(meta, queries, kv, kv)


def output_kernel(c_ref, w_ref, o_ref):
    o_ref[0] = jnp.dot(c_ref[...], w_ref[...], preferred_element_type=jnp.float32).astype(jnp.bfloat16)


def output_terms(context, out_weight, shards):
    rows, head_width = context.shape
    width = out_weight.shape[1] // shards
    return pl.pallas_call(
        output_kernel,
        grid=(shards,),
        out_shape=jax.ShapeDtypeStruct((shards, rows, width), jnp.bfloat16),
        in_specs=[
            pl.BlockSpec((rows, head_width), lambda z: (0, 0)),
            pl.BlockSpec((head_width, width), lambda z: (0, z)),
        ],
        out_specs=pl.BlockSpec((1, rows, width), lambda z: (z, 0, 0)),
        compiler_params=pltpu.CompilerParams(vmem_limit_bytes=VMEM_LIMIT),
        name="output_terms",
    )(context, out_weight)


def per_device(hidden, depth, qkv_weight, out_weight):
    tokens = hidden[0]
    local_len = tokens.shape[0]
    docs = lax.axis_size("dp")
    ctx_count = lax.axis_size("ctx")
    shards = lax.axis_size("tensor")
    plane = docs * ctx_count
    me = lax.axis_index("dp") * ctx_count + lax.axis_index("ctx")
    size = CAP // plane
    stripes = ACT_DEV // size

    active = depth[0] >= RECURSION
    ones = active.astype(jnp.int32)
    counts = lax.all_gather(jnp.sum(ones)[None], PLANE, axis=0, tiled=True)
    ends = jnp.cumsum(counts)
    starts = ends - counts
    rank = jnp.cumsum(ones) - 1
    slot = jnp.where(active, lax.rem(starts[me] + rank, CAP), -1)
    onehot = (jnp.arange(CAP, dtype=jnp.int32)[:, None] == slot[None, :]).astype(jnp.bfloat16)
    dealt = jnp.dot(onehot, tokens, preferred_element_type=jnp.float32).astype(jnp.bfloat16)
    received = lax.all_to_all(dealt.reshape(plane, size, -1), PLANE, 0, 0)

    index = (
        jnp.arange(stripes, dtype=jnp.int32)[:, None] * CAP
        + me * size
        + jnp.arange(size, dtype=jnp.int32)[None, :]
    )
    owned = (index[None] >= starts[:, None, None]) & (index[None] < ends[:, None, None])
    zero = jnp.zeros((), jnp.bfloat16)
    packed = jnp.where(owned[0][:, :, None], received[0][None], zero)
    for b in range(1, plane):
        packed = jnp.where(owned[b][:, :, None], received[b][None], packed)
    packed = packed.reshape(ACT_DEV, -1)

    rows_all = lax.all_gather(packed, "tensor", axis=0)
    weight = jnp.transpose(qkv_weight, (1, 0, 2))
    projected = project(rows_all, weight)
    kv = lax.all_gather(projected[1:], PLANE, axis=0)
    meta = jnp.concatenate([starts[::ctx_count], me[None]]).astype(jnp.int32)
    context = attend(meta, projected[0], kv, docs, stripes)
    terms = output_terms(context, out_weight, shards)
    rows_back = lax.psum_scatter(terms, "tensor", scatter_dimension=0)

    rows_back = rows_back.reshape(stripes, size, -1)
    returned = jnp.where(owned[:, 0][:, :, None], rows_back[0][None], zero)
    for k in range(1, stripes):
        returned = jnp.where(owned[:, k][:, :, None], rows_back[k][None], returned)
    landed = lax.all_to_all(returned, PLANE, 0, 0).reshape(CAP, -1)
    spread = (slot[:, None] == jnp.arange(CAP, dtype=jnp.int32)[None, :]).astype(jnp.bfloat16)
    update = jnp.dot(spread, landed, preferred_element_type=jnp.float32).astype(jnp.bfloat16)
    return update[None]


def solution(mesh):
    placed = (P("dp", "ctx", "tensor"), P("dp", "ctx"), P(None, None, "tensor"), P("tensor", None))
    return jax.shard_map(
        per_device, mesh=mesh, in_specs=placed, out_specs=P("dp", "ctx", "tensor"), check_vma=False
    )
```

time: 480 us -> 313 us (0.65)
  local copies, waits for them, and re-layouts: 123 us -> 9.92 us
  matrix products: 88 us -> 20.2 us
  Pallas kernels: 0 us -> 44.4 us
  other arithmetic: 35.6 us -> 6.79 us
  waiting for transfers between devices: 210 us -> 184 us
  blocking collectives: 7.93 us -> 30.4 us
    unnamed x4 -> x3, waiting for transfers between devices: 94 us -> 0.05 us
    dot_general x4 -> x2, matrix products: 88 us -> 20.2 us  [the longest x1 10.8 us: per_device(): jnp.dot(onehot, tokens, preferred_element_type=jnp.float32)]
    reduce_scatter x0 -> x1, waiting for transfers between devices: none -> 52.4 us  [per_device(): rows_back = lax.psum_scatter(terms, 'tensor', scatter_dimension=0)]
    pallas_call x0 -> x3, Pallas kernels: none -> 44.4 us  [the longest x1 26.2 us: attend(): pl.pallas_call(functools.partial(attend_kernel, docs), grid_spec=pltpu.Pr...]
    gather x3 -> x0, local copies, waits for them, and re-layouts: 25.8 us -> none  [the longest x1 16.7 us: per_device(): slot_token[source_slot][None, :] <= slot_token[:, None]]
    scatter x2 -> x0, local copies, waits for them, and re-layouts: 24.5 us -> none  [the longest x1 15.5 us: per_device(): slot_token = jnp.zeros((capacity,), jnp.int32).at[jnp.where(active > 0, a...]
    unnamed x14 -> x3, local copies, waits for them, and re-layouts: 27.1 us -> 2.76 us
    slice x5 -> x4, local copies, waits for them, and re-layouts: 26.4 us -> 2.73 us  [the longest x1 2.5 us: per_device(): kv = lax.all_gather(projected[1:], PLANE, axis=0)]
  transfers between devices with their start and end apart: 3 -> 4, of which waited for: 3 -> 4; matrix products, arithmetic and copies ran while one was open for 9% -> 1% of each run, Pallas kernels for 0% -> 0%
where the time goes in v1:
time: 313 us
  waiting for transfers between devices  184 us (59%)
  Pallas kernels  44.4 us (14%)
  blocking collectives  30.4 us (10%)
  matrix products  20.2 us (6%)
  between operations  13.2 us (4%)
  local copies, waits for them, and re-layouts  9.92 us (3%)
  other arithmetic  6.79 us (2%)
  starting transfers between devices  3.88 us (1%)
    all_gather x1, waiting for transfers between devices, per_device(): kv = lax.all_gather(projected[1:], PLANE, axis=0)  59.3 us
    all_gather x1, waiting for transfers between devices, per_device(): rows_all = lax.all_gather(packed, 'tensor', axis=0)  54.9 us
    reduce_scatter x1, waiting for transfers between devices, per_device(): rows_back = lax.psum_scatter(terms, 'tensor', scatter_dimension=0)  52.4 us
    pallas_call x1, Pallas kernels, attend(): pl.pallas_call(functools.partial(attend_kernel, docs), grid_spec=pltpu.Pr...  26.2 us
    all_to_all x1, blocking collectives, per_device(): landed = lax.all_to_all(returned, PLANE, 0, 0).reshape(CAP, -1)  20.9 us
    all_to_all x1, waiting for transfers between devices, per_device(): received = lax.all_to_all(dealt.reshape(plane, size, -1), PLANE, 0, 0)  16.9 us
    pallas_call x1, Pallas kernels, project(): pl.pallas_call(project_kernel, grid=(3,), out_shape=jax.ShapeDtypeStruct(...  12.4 us
    dot_general x1, matrix products, per_device(): jnp.dot(onehot, tokens, preferred_element_type=jnp.float32)  10.8 us
  transfers between devices with their start and end apart: 4, of which 4 were waited for; matrix products, arithmetic and copies ran while one was open for 1% of the time, Pallas kernels for 0%

profile of v1, /device:TPU:0, one launch (start us, length us, event | category | flops | bytes accessed | tf_op | source)
XLA Modules:
  0.0 312.5 jit_solution(9179271349490020165)
XLA Ops:
  6.5 0.8 fusion.21
  7.3 0.6 convert_reduce_fusion
  8.0 1.3 dynamic-slice
  9.3 1.4 dynamic-update-slice
  10.7 9.5 %all-reduce = s32[8]{0:T(128)S(1)} all-reduce(s32[8]{0:T(128)S(1)} %dynamic-update-slice), channel_id=1, replica_groups=mesh['dp'=2,'ctx'=4,'tensor'=4] {'dp','ctx'}, use_global_device_ids=true, to_apply=%add | all-reduce | flops 8 | bytes 64
  21.5 0.7 fusion.18
  22.2 0.8 fusion.20
  23.0 10.8 %fusion.7 = bf16[1024,640]{1,0:T(8,128)(2,1)} fusion(bf16[1,4096,640]{2,1,0:T(8,128)(2,1)} %param.4, s32[4096]{0:T(1024)S(1)} %bitcast.118), kind=kOutput, calls=%fused_computation.9 | convolution fusion | flops 5373558784 | bytes 6569984 | tf_op jit(solution)/shard_map/dot_general | solution.py:160
  33.8 3.6 %all-to-all-start = ((bf16[8,128,640]{2,1,0:T(8,128)(2,1)}), bf16[8,128,640]{2,1,0:T(8,128)(2,1)S(1)}, u32[]{:S(2)}, u32[]{:S(2)}) async-start(bf16[8,128,640]{2,1,0:T(8,128)(2,1)} %bitcast.12), calls=%async_computation | async-start | bytes 2621440 | tf_op jit(solution)/shard_map/all_to_all | solution.py:161
  37.6 16.9 %all-to-all-done = bf16[8,128,640]{2,1,0:T(8,128)(2,1)S(1)} async-done(((bf16[8,128,640]{2,1,0:T(8,128)(2,1)}), bf16[8,128,640]{2,1,0:T(8,128)(2,1)S(1)}, u32[]{:S(2)}, u32[]{:S(2)}) %all-to-all-start) | async-done | bytes 1310752 | tf_op jit(solution)/shard_map/all_to_all | solution.py:161
  55.2 1.7 fusion.16
  57.1 54.9 %all-gather.4.cloned.1.call-done.x_ref = bf16[4,512,640]{2,1,0:T(8,128)(2,1)} async-done(((bf16[1,512,640]{2,1,0:T(8,128)(2,1)}), bf16[4,512,640]{2,1,0:T(8,128)(2,1)}) %all-gather.4.cloned.1.call-update) | async-done | bytes 2621456 | tf_op jit(solution)/shard_map/all_gather | solution.py:175
  112.1 12.4 %project.1 = bf16[3,512,640]{2,1,0:T(8,128)(2,1)} custom-call(bf16[4,512,640]{2,1,0:T(8,128)(2,1)} %all-gather.4.cloned.1.call-done.x_ref, bf16[3,2560,640]{2,1,0:T(8,128)(2,1)} %bitcast.106), custom_call_target="tpu_custom_call" | custom-call | tf_op jit(solution)/shard_map/project/pallas_call | solution.py:50
  124.5 2.5 slice.141
  127.1 0.6 pad_add_fusion.meta_ref
  127.7 2.0 slice_bitcast_fusion.q_ref
  129.7 59.3 %all-gather.6.cloned.1.call-done = bf16[16,512,640]{2,1,0:T(8,128)(2,1)} async-done(((bf16[2,512,640]{2,1,0:T(8,128)(2,1)}), bf16[16,512,640]{2,1,0:T(8,128)(2,1)}) %all-gather.6.cloned.1.call-update) | async-done | bytes 10485776 | tf_op jit(solution)/shard_map/all_gather | solution.py:178
  189.0 26.2 %attend.1.c_ref = bf16[512,640]{1,0:T(8,128)(2,1)} custom-call(s32[3]{0:T(128)} %pad_add_fusion.meta_ref, bf16[512,640]{1,0:T(8,128)(2,1)} %slice_bitcast_fusion.q_ref, bf16[8,2,4,128,640]{4,3,2,1,0:T(8,128)(2,1)} %bitcast.104, bf16[8,2,4,128,640]{4,3,2,1,0:T(8,128)(2,1)} %bitcast.105), custom_call_target="tpu_custom_call" | custom-call | tf_op jit(solution)/shard_map/attend/pallas_call | solution.py:102
  215.2 5.9 %output_terms.1 = bf16[4,512,640]{2,1,0:T(8,128)(2,1)} custom-call(bf16[512,640]{1,0:T(8,128)(2,1)} %attend.1.c_ref, bf16[640,2560]{1,0:T(8,128)(2,1)} %w_ref.1), custom_call_target="tpu_custom_call" | custom-call | tf_op jit(solution)/shard_map/output_terms/pallas_call | solution.py:127
  221.1 52.4 %reduce-scatter.2.cloned.1.call-done = bf16[1,512,640]{2,1,0:T(8,128)(2,1)} async-done(((bf16[4,512,640]{2,1,0:T(8,128)(2,1)}), bf16[1,512,640]{2,1,0:T(8,128)(2,1)}) %reduce-scatter.2.cloned.1.call-update) | async-done | bytes 655376 | tf_op jit(solution)/shard_map/reduce_scatter | solution.py:182
  273.5 1.2 slice_bitcast_fusion.4
  274.7 0.9 select_select_fusion
  275.7 20.9 %all_to_all.10 = bf16[8,128,640]{2,1,0:T(8,128)(2,1)S(1)} all-to-all(bf16[8,128,640]{2,1,0:T(8,128)(2,1)S(1)} %select_select_fusion), channel_id=1, replica_groups=mesh['dp'=2,'ctx'=4,'tensor'=4] {'dp','ctx'}, dimensions={0} | all-to-all | bytes 2621440 | tf_op jit(solution)/shard_map/all_to_all | solution.py:188
  296.6 9.4 %fusion.5 = bf16[1,4096,640]{2,1,0:T(8,128)(2,1)} fusion(bf16[1024,640]{1,0:T(8,128)(2,1)S(1)} %bitcast.115, s32[4096]{0:T(1024)S(1)} %get-tuple-element.13), kind=kOutput, calls=%fused_computation.7 | convolution fusion | flops 5375524864 | bytes 6569984 | tf_op jit(solution)/shard_map/dot_general | solution.py:190
  (29 shorter events, 2.5 us)
Async XLA Ops:
  33.8 20.8 %all-to-all-start = ((bf16[8,128,640]{2,1,0:T(8,128)(2,1)}), bf16[8,128,640]{2,1,0:T(8,128)(2,1)S(1)}, u32[]{:S(2)}, u32[]{:S(2)}) async-start(bf16[8,128,640]{2,1,0:T(8,128)(2,1)} %bitcast.12), calls=%async_computation | async-start | bytes 2621440 | tf_op jit(solution)/shard_map/all_to_all | solution.py:161
  37.4 74.7 %all-gather.4.cloned.1.call-start = ((), (), s32[]{:S(2)}) async-start(), calls=%async_computation.3 | async-start | bytes 3276800 | tf_op jit(solution)/shard_map/all_gather | solution.py:175
  56.9 132.1 %all-gather.6.cloned.1.call-start = ((), (), s32[]{:S(2)}) async-start(), calls=%async_computation.5 | async-start | bytes 11796480 | tf_op jit(solution)/shard_map/all_gather | solution.py:178
  127.0 146.5 %reduce-scatter.2.cloned.1.call-start = ((), (), s32[]{:S(2)}) async-start(), calls=%async_computation.4 | async-start | bytes 3276800 | tf_op jit(solution)/shard_map/reduce_scatter | solution.py:182
Sparse Core Ops, SparseCore 0:
  57.0 55.0 all-gather.3
  127.1 61.8 all-gather.5
  221.2 52.2 reduce-scatter.1

commit v2 on v1

--- a/solution.py
+++ b/solution.py
@@ -19,7 +19,7 @@
 PLANE = ("dp", "ctx")
 
 
-def project_kernel(x_ref, w_ref, o_ref, normed):
+def project_kernel(x_ref, w_ref, q_ref, kv_ref, normed):
     part = pl.program_id(0)
     shards, rows, width = x_ref.shape
 
@@ -36,85 +36,215 @@
     acc = jnp.dot(normed[0], w_ref[0, :width], preferred_element_type=jnp.float32)
     for z in range(1, shards):
         acc = acc + jnp.dot(normed[z], w_ref[0, z * width : (z + 1) * width], preferred_element_type=jnp.float32)
-    scale = jnp.where(part == 0, score_scale, 1.0)
-    for h in range(acc.shape[1] // HD):
-        head = acc[:, h * HD : (h + 1) * HD]
-        factor = lax.rsqrt(jnp.mean(head * head, axis=1, keepdims=True) + head_epsilon) * scale
-        factor = jnp.where(part == 2, 1.0, factor)
-        o_ref[0, :, h * HD : (h + 1) * HD] = (head * factor).astype(jnp.bfloat16)
+    heads = acc.shape[1] // HD
+
+    def head_normed(scale):
+        parts = []
+        for h in range(heads):
+            head = acc[:, h * HD : (h + 1) * HD]
+            factor = lax.rsqrt(jnp.mean(head * head, axis=1, keepdims=True) + head_epsilon) * scale
+            parts.append((head * factor).astype(jnp.bfloat16))
+        return parts
+
+    @pl.when(part == 0)
+    def _():
+        for h, value in enumerate(head_normed(score_scale)):
+            q_ref[:, h * HD : (h + 1) * HD] = value
+
+    @pl.when(part == 1)
+    def _():
+        for h, value in enumerate(head_normed(1.0)):
+            kv_ref[0, :, h * HD : (h + 1) * HD] = value
+
+    @pl.when(part == 2)
+    def _():
+        kv_ref[0] = acc.astype(jnp.bfloat16)
 
 
 def project(rows_all, weight):
     shards, rows, width = rows_all.shape
     head_width = weight.shape[2]
+    flops = 2 * rows * shards * width * 3 * head_width
     return pl.pallas_call(
         project_kernel,
         grid=(3,),
-        out_shape=jax.ShapeDtypeStruct((3, rows, head_width), jnp.bfloat16),
+        out_shape=[
+            jax.ShapeDtypeStruct((rows, head_width), jnp.bfloat16),
+            jax.ShapeDtypeStruct((2, rows, head_width), jnp.bfloat16),
+        ],
         in_specs=[
             pl.BlockSpec((shards, rows, width), lambda p: (0, 0, 0)),
             pl.BlockSpec((1, shards * width, head_width), lambda p: (p, 0, 0)),
         ],
-        out_specs=pl.BlockSpec((1, rows, head_width), lambda p: (p, 0, 0)),
+        out_specs=[
+            pl.BlockSpec((rows, head_width), lambda p: (0, 0)),
+            pl.BlockSpec((1, rows, head_width), lambda p: (jnp.maximum(p - 1, 0), 0, 0)),
+        ],
         scratch_shapes=[pltpu.VMEM((shards, rows, width), jnp.bfloat16)],
         compiler_params=pltpu.CompilerParams(vmem_limit_bytes=VMEM_LIMIT),
+        cost_estimate=pl.CostEstimate(flops=flops, bytes_accessed=2 * weight.size, transcendentals=0),
         name="project",
     )(rows_all, weight)
 
 
-def attend_kernel(docs, meta_ref, q_ref, k_ref, v_ref, o_ref):
-    stripe = pl.program_id(1)
-    plane, stripes, size, _ = k_ref.shape
+def gather_kernel(pieces, kv_ref, out_ref, send_sem, recv_sem, local_sem):
+    x, place = lax.axis_index("dp"), lax.axis_index("ctx")
+    y, core = place // 2, lax.rem(place, 2)
+    rows = kv_ref.shape[1] // pieces
+
+    def block(flip_x, flip_y, flip_core):
+        return (x ^ flip_x) * 4 + (y ^ flip_y) * 2 + (core ^ flip_core)
+
+    def device(flip_x, flip_y, flip_core):
+        return {"dp": x ^ flip_x, "ctx": (y ^ flip_y) * 2 + (core ^ flip_core)}
+
+    sibling, across_x, across_y = device(0, 0, 1), device(1, 0, 0), device(0, 1, 0)
+    barrier = pltpu.get_barrier_semaphore()
+    for target in (sibling, across_x, across_y):
+        pl.semaphore_signal(barrier, inc=1, device_id=target, device_id_type=pl.DeviceIdType.MESH)
+    pl.semaphore_wait(barrier, 3)
+
+    me = block(0, 0, 0)
+    local = pltpu.make_async_copy(kv_ref, out_ref.at[me], local_sem)
+    local.start()
+    sends = []
+
+    def send(origin, route, piece, target, own=False):
+        window = pl.ds(piece * rows, rows)
+        copy = pltpu.make_async_remote_copy(
+            src_ref=kv_ref.at[:, window] if own else out_ref.at[origin, :, window],
+            dst_ref=out_ref.at[origin, :, window],
+            send_sem=send_sem.at[route, piece],
+            recv_sem=recv_sem.at[route, piece],
+            device_id=target,
+            device_id_type=pl.DeviceIdType.MESH,
+        )
+        copy.start()
+        sends.append(copy)
+
+    def arrive(origin, route, piece):
+        window = pl.ds(piece * rows, rows)
+        pltpu.make_async_remote_copy(
+            src_ref=out_ref.at[origin, :, window],
+            dst_ref=out_ref.at[origin, :, window],
+            send_sem=send_sem.at[route, piece],
+            recv_sem=recv_sem.at[route, piece],
+            device_id=sibling,
+            device_id_type=pl.DeviceIdType.MESH,
+        ).wait_recv()
+
+    for piece in range(pieces):
+        send(me, 1, piece, across_x, True)
+        send(me, 2, piece, across_y, True)
+        send(me, 0, piece, sibling, True)
+    first = core == 0
+    onward = jnp.where(first, block(0, 1, 0), block(1, 0, 0))
+    onward_device = {
+        "dp": jnp.where(first, x ^ 1, x),
+        "ctx": jnp.where(first, place, (y ^ 1) * 2 + core),
+    }
+    for piece in range(pieces):
+        arrive(block(1, 0, 0), 1, piece)
+        arrive(block(0, 1, 0), 2, piece)
+        send(onward, 3, piece, onward_device)
+        send(block(1, 0, 0), 4, piece, sibling)
+        send(block(0, 1, 0), 5, piece, sibling)
+    for piece in range(pieces):
+        arrive(block(1, 1, 0), 3, piece)
+        send(block(1, 1, 0), 6, piece, sibling)
+    for piece in range(pieces):
+        arrive(block(0, 0, 1), 0, piece)
+        arrive(block(1, 0, 1), 4, piece)
+        arrive(block(0, 1, 1), 5, piece)
+        arrive(block(1, 1, 1), 6, piece)
+    for copy in sends:
+        copy.wait_send()
+    local.wait()
+
+
+def gather_plane(kv, call):
+    docs, ctx_count = lax.axis_size("dp"), lax.axis_size("ctx")
+    if (docs, ctx_count) != (2, 4):
+        return lax.all_gather(kv, PLANE, axis=0)
+    pieces = 4
+    plane = docs * ctx_count
+    return pl.pallas_call(
+        functools.partial(gather_kernel, pieces),
+        out_shape=jax.ShapeDtypeStruct((plane,) + kv.shape, kv.dtype),
+        in_specs=[pl.BlockSpec(memory_space=pltpu.VMEM)],
+        out_specs=pl.BlockSpec(memory_space=pl.ANY),
+        scratch_shapes=[
+            pltpu.SemaphoreType.DMA((7, pieces)),
+            pltpu.SemaphoreType.DMA((7, pieces)),
+            pltpu.SemaphoreType.DMA,
+        ],
+        compiler_params=pltpu.CompilerParams(collective_id=call, has_side_effects=True),
+        cost_estimate=pl.CostEstimate(flops=0, bytes_accessed=60_000_000, transcendentals=0),
+        name="gather_plane",
+    )(kv)
+
+
+def attend_kernel(docs, base, meta_ref, q_ref, *refs):
+    o_ref = refs[-1]
+    pairs = [(refs[i], refs[i + 1]) for i in range(0, len(refs) - 1, 2)]
+    plane, stripes, size, _ = refs[0].shape
     period = plane * size
+    rows = stripes * size
     me = meta_ref[docs]
-    query = q_ref[...]
-    q_index = stripe * period + me * size + lax.broadcasted_iota(jnp.int32, (size, 1), 0)
-    begin = jnp.zeros((size, 1), jnp.int32)
+    row = lax.broadcasted_iota(jnp.int32, (rows, 1), 0)
+    q_index = (base + row // size) * period + me * size + lax.rem(row, size)
+    begin = jnp.zeros((rows, 1), jnp.int32)
     for d in range(docs):
         begin = jnp.where(q_index >= meta_ref[d], meta_ref[d], begin)
-    lane = lax.broadcasted_iota(jnp.int32, (size, period), 1)
-
-    def tile(at, carry, diagonal):
-        num, den = carry
-        keys = k_ref[:, pl.ds(at, 1)].reshape(period, HD)
-        values = v_ref[:, pl.ds(at, 1)].reshape(period, HD)
-        scores = lax.dot_general(query, keys, (((1,), (1,)), ((), ())), preferred_element_type=jnp.float32)
-        allowed = lane >= begin - at * period
-        if diagonal:
-            allowed = allowed & (lane <= q_index - at * period)
-        weights = jnp.where(allowed, jnp.exp(scores), 0.0)
-        den = den + jnp.sum(weights, axis=1, keepdims=True)
-        num = num + jnp.dot(weights.astype(jnp.bfloat16), values, preferred_element_type=jnp.float32)
-        return num, den
-
-    carry = (jnp.zeros((size, HD), jnp.float32), jnp.zeros((size, 1), jnp.float32))
-    carry = lax.fori_loop(0, stripe, lambda at, c: tile(at, c, False), carry)
-    num, den = tile(stripe, carry, True)
+    lane = lax.broadcasted_iota(jnp.int32, (1, period), 1)
+    query = q_ref[...]
+    num = jnp.zeros((rows, HD), jnp.float32)
+    den = jnp.zeros((rows, 1), jnp.float32)
+    at = 0
+    for k_ref, v_ref in pairs:
+        for k in range(stripes):
+            keys = k_ref[:, k].reshape(period, HD)
+            values = v_ref[:, k].reshape(period, HD)
+            scores = lax.dot_general(query, keys, (((1,), (1,)), ((), ())), preferred_element_type=jnp.float32)
+            allowed = lane >= begin - at * period
+            if at >= base:
+                allowed = allowed & (lane <= q_index - at * period)
+            weights = jnp.where(allowed, jnp.exp(scores), 0.0)
+            den = den + jnp.sum(weights, axis=1, keepdims=True)
+            num = num + jnp.dot(weights.astype(jnp.bfloat16), values, preferred_element_type=jnp.float32)
+            at += 1
     o_ref[...] = (num / den).astype(jnp.bfloat16)
 
 
-def attend(meta, queries, kv, docs, stripes):
+def attend(meta, queries, kvs, docs, stripes):
     rows, head_width = queries.shape
-    plane = kv.shape[0]
+    plane = kvs[0].shape[0]
     size = rows // stripes
     heads = head_width // HD
-    kv = kv.reshape(plane, 2, stripes, size, head_width)
+    operands, specs = [], []
+    for kv in kvs:
+        kv = kv.reshape(plane, 2, stripes, size, head_width)
+        for which in range(2):
+            operands.append(kv)
+            specs.append(
+                pl.BlockSpec((plane, None, stripes, size, HD), lambda h, m, which=which: (0, which, 0, 0, h))
+            )
+    pairs = rows * plane * rows * len(kvs)
     return pl.pallas_call(
-        functools.partial(attend_kernel, docs),
+        functools.partial(attend_kernel, docs, (len(kvs) - 1) * stripes),
         grid_spec=pltpu.PrefetchScalarGridSpec(
             num_scalar_prefetch=1,
-            grid=(heads, stripes),
-            in_specs=[
-                pl.BlockSpec((size, HD), lambda h, k, m: (k, h)),
-                pl.BlockSpec((plane, None, stripes, size, HD), lambda h, k, m: (0, 0, 0, 0, h)),
-                pl.BlockSpec((plane, None, stripes, size, HD), lambda h, k, m: (0, 1, 0, 0, h)),
-            ],
-            out_specs=pl.BlockSpec((size, HD), lambda h, k, m: (k, h)),
+            grid=(heads,),
+            in_specs=[pl.BlockSpec((rows, HD), lambda h, m: (0, h))] + specs,
+            out_specs=pl.BlockSpec((rows, HD), lambda h, m: (0, h)),
         ),
         out_shape=jax.ShapeDtypeStruct((rows, head_width), jnp.bfloat16),
         compiler_params=pltpu.CompilerParams(vmem_limit_bytes=VMEM_LIMIT),
+        cost_estimate=pl.CostEstimate(
+            flops=4 * pairs * head_width, bytes_accessed=4 * kvs[0].size, transcendentals=pairs * heads
+        ),
         name="attend",
-    )(meta, queries, kv, kv)
+    )(meta, queries, *operands)
 
 
 def output_kernel(c_ref, w_ref, o_ref):
@@ -172,14 +302,22 @@
         packed = jnp.where(owned[b][:, :, None], received[b][None], packed)
     packed = packed.reshape(ACT_DEV, -1)
 
-    rows_all = lax.all_gather(packed, "tensor", axis=0)
+    chunks = 2
+    chunk_stripes = stripes // chunks
+    chunk_rows = ACT_DEV // chunks
     weight = jnp.transpose(qkv_weight, (1, 0, 2))
-    projected = project(rows_all, weight)
-    kv = lax.all_gather(projected[1:], PLANE, axis=0)
     meta = jnp.concatenate([starts[::ctx_count], me[None]]).astype(jnp.int32)
-    context = attend(meta, projected[0], kv, docs, stripes)
-    terms = output_terms(context, out_weight, shards)
-    rows_back = lax.psum_scatter(terms, "tensor", scatter_dimension=0)
+    rows_all = [
+        lax.all_gather(packed[c * chunk_rows : (c + 1) * chunk_rows], "tensor", axis=0) for c in range(chunks)
+    ]
+    kvs, backs = [], []
+    for c in range(chunks):
+        queries, kv = project(rows_all[c], weight)
+        kvs.append(gather_plane(kv, c))
+        context = attend(meta, queries, kvs, docs, chunk_stripes)
+        terms = output_terms(context, out_weight, shards)
+        backs.append(lax.psum_scatter(terms, "tensor", scatter_dimension=0))
+    rows_back = jnp.concatenate(backs, axis=0)
 
     rows_back = rows_back.reshape(stripes, size, -1)
     returned = jnp.where(owned[:, 0][:, :, None], rows_back[0][None], zero)

time: 313 us -> 263 us (0.84)
  waiting for transfers between devices: 184 us -> 78.1 us
  Pallas kernels: 44.4 us -> 104 us
  local copies, waits for them, and re-layouts: 9.92 us -> 6.63 us
    all_gather x2, waiting for transfers between devices: 114 us -> 31.3 us  [per_device(): lax.all_gather(packed[c * chunk_rows:(c + 1) * chunk_rows], 'tensor', axi...]
    pallas_call x2 -> x6, Pallas kernels: 38.5 us -> 93.9 us  [the longest x2 54.3 us: gather_plane(): pl.pallas_call(functools.partial(gather_kernel, pieces), out_shape=jax.Sh...]
    reduce_scatter x1 -> x2, waiting for transfers between devices: 52.4 us -> 29.2 us  [per_device(): backs.append(lax.psum_scatter(terms, 'tensor', scatter_dimension=0))]
    pallas_call x1 -> x2, Pallas kernels: 5.9 us -> 9.61 us  [output_terms(): pl.pallas_call(output_kernel, grid=(shards,), out_shape=jax.ShapeDtypeStr...]
  transfers between devices with their start and end apart: 4 -> 5, of which waited for: 4 -> 3; matrix products, arithmetic and copies ran while one was open for 1% -> 1% of each run, Pallas kernels for 0% -> 39%
where the time goes in v2:
time: 263 us; the launch traced here: 262 us
  Pallas kernels  104 us (40%)
  waiting for transfers between devices  78.1 us (30%)
  blocking collectives  30.4 us (12%)
  matrix products  20.2 us (8%)
  between operations  13.3 us (5%)
  local copies, waits for them, and re-layouts  6.63 us (3%)
  other arithmetic  6.11 us (2%)
  starting transfers between devices  3.91 us (1%)
    pallas_call x2, Pallas kernels, gather_plane(): pl.pallas_call(functools.partial(gather_kernel, pieces), out_shape=jax.Sh...  54.3 us
    all_gather x2, waiting for transfers between devices, per_device(): lax.all_gather(packed[c * chunk_rows:(c + 1) * chunk_rows], 'tensor', axi...  31.3 us
    reduce_scatter x2, waiting for transfers between devices, per_device(): backs.append(lax.psum_scatter(terms, 'tensor', scatter_dimension=0))  29.2 us
    pallas_call x2, Pallas kernels, attend(): pl.pallas_call(functools.partial(attend_kernel, docs, (len(kvs) - 1) * st...  22.5 us
    all_to_all x1, blocking collectives, per_device(): landed = lax.all_to_all(returned, PLANE, 0, 0).reshape(CAP, -1)  20.9 us
    pallas_call x2, Pallas kernels, project(): pl.pallas_call(project_kernel, grid=(3,), out_shape=[jax.ShapeDtypeStruct...  17.2 us
    all_to_all x1, waiting for transfers between devices, per_device(): received = lax.all_to_all(dealt.reshape(plane, size, -1), PLANE, 0, 0)  16.9 us
    dot_general x1, matrix products, per_device(): jnp.dot(onehot, tokens, preferred_element_type=jnp.float32)  10.8 us
  transfers between devices with their start and end apart: 5, of which 3 were waited for; matrix products, arithmetic and copies ran while one was open for 1% of the time, Pallas kernels for 39%

profile of v2, /device:TPU:0, one launch (start us, length us, event | category | flops | bytes accessed | tf_op | source)
XLA Modules:
  0.0 262.2 jit_solution(5568834005846775505)
XLA Ops:
  6.5 0.8 fusion.14
  8.0 1.3 dynamic-slice
  9.2 1.4 dynamic-update-slice
  10.6 9.5 %all-reduce = s32[8]{0:T(128)S(1)} all-reduce(s32[8]{0:T(128)S(1)} %dynamic-update-slice), channel_id=1, replica_groups=mesh['dp'=2,'ctx'=4,'tensor'=4] {'dp','ctx'}, use_global_device_ids=true, to_apply=%add | all-reduce | flops 8 | bytes 64
  22.9 10.8 %fusion.7 = bf16[1024,640]{1,0:T(8,128)(2,1)} fusion(bf16[1,4096,640]{2,1,0:T(8,128)(2,1)} %param.4, s32[4096]{0:T(1024)S(1)} %bitcast.88), kind=kOutput, calls=%fused_computation.9 | convolution fusion | flops 5373558784 | bytes 6569984 | tf_op jit(solution)/shard_map/dot_general | solution.py:290
  33.7 3.6 %all-to-all-start = ((bf16[8,128,640]{2,1,0:T(8,128)(2,1)}), bf16[8,128,640]{2,1,0:T(8,128)(2,1)S(1)}, u32[]{:S(2)}, u32[]{:S(2)}) async-start(bf16[8,128,640]{2,1,0:T(8,128)(2,1)} %bitcast.12), calls=%async_computation | async-start | bytes 2621440 | tf_op jit(solution)/shard_map/all_to_all | solution.py:291
  37.6 16.9 %all-to-all-done = bf16[8,128,640]{2,1,0:T(8,128)(2,1)S(1)} async-done(((bf16[8,128,640]{2,1,0:T(8,128)(2,1)}), bf16[8,128,640]{2,1,0:T(8,128)(2,1)S(1)}, u32[]{:S(2)}, u32[]{:S(2)}) %all-to-all-start) | async-done | bytes 1310752 | tf_op jit(solution)/shard_map/all_to_all | solution.py:291
  54.6 1.0 select_select_fusion.1
  55.6 0.9 fusion.16
  58.2 31.3 %all-gather.5.cloned.1.call-done.x_ref = bf16[4,256,640]{2,1,0:T(8,128)(2,1)} async-done(((bf16[1,256,640]{2,1,0:T(8,128)(2,1)}), bf16[4,256,640]{2,1,0:T(8,128)(2,1)}) %all-gather.5.cloned.1.call-update) | async-done | bytes 1310736 | tf_op jit(solution)/shard_map/all_gather | solution.py:311
  89.4 8.5 %project.3 = (bf16[256,640]{1,0:T(8,128)(2,1)}, bf16[2,256,640]{2,1,0:T(8,128)(2,1)}) custom-call(bf16[4,256,640]{2,1,0:T(8,128)(2,1)} %all-gather.5.cloned.1.call-done.x_ref, bf16[3,2560,640]{2,1,0:T(8,128)(2,1)} %bitcast.81), custom_call_target="tpu_custom_call" | custom-call | flops 2516582400 | bytes 9830400 | tf_op jit(solution)/shard_map/project/pallas_call | solution.py:68
  97.9 27.0 %gather_plane.2 = bf16[8,2,256,640]{3,2,1,0:T(8,128)(2,1)} custom-call(bf16[2,256,640]{2,1,0:T(8,128)(2,1)} %get-tuple-element.10.kv_ref), custom_call_target="tpu_custom_call" | custom-call | bytes 60000000 | tf_op jit(solution)/shard_map/gather_plane/pallas_call | solution.py:171
  125.0 8.9 %attend.3.c_ref = bf16[256,640]{1,0:T(8,128)(2,1)} custom-call(s32[3]{0:T(128)} %pad_add_fusion.meta_ref, bf16[256,640]{1,0:T(8,128)(2,1)} %get-tuple-element.12.q_ref, bf16[8,2,2,128,640]{4,3,2,1,0:T(8,128)(2,1)} %bitcast.75, bf16[8,2,2,128,640]{4,3,2,1,0:T(8,128)(2,1)} %bitcast.76), custom_call_target="tpu_custom_call" | custom-call | flops 1342177280 | bytes 10485760 | tf_op jit(solution)/shard_map/attend/pallas_call | solution.py:233
  133.9 4.8 %output_terms.3 = bf16[4,256,640]{2,1,0:T(8,128)(2,1)} custom-call(bf16[256,640]{1,0:T(8,128)(2,1)} %attend.3.c_ref, bf16[640,2560]{1,0:T(8,128)(2,1)} %w_ref.3), custom_call_target="tpu_custom_call" | custom-call | tf_op jit(solution)/shard_map/output_terms/pallas_call | solution.py:257
  138.7 8.7 %project.2 = (bf16[256,640]{1,0:T(8,128)(2,1)}, bf16[2,256,640]{2,1,0:T(8,128)(2,1)}) custom-call(bf16[4,256,640]{2,1,0:T(8,128)(2,1)} %all-gather.3.cloned.1.call-done.x_ref, bf16[3,2560,640]{2,1,0:T(8,128)(2,1)} %bitcast.82), custom_call_target="tpu_custom_call" | custom-call | flops 2516582400 | bytes 9830400 | tf_op jit(solution)/shard_map/project/pallas_call | solution.py:68
  147.4 27.3 %gather_plane.3 = bf16[8,2,256,640]{3,2,1,0:T(8,128)(2,1)} custom-call(bf16[2,256,640]{2,1,0:T(8,128)(2,1)} %get-tuple-element.11.kv_ref), custom_call_target="tpu_custom_call" | custom-call | bytes 60000000 | tf_op jit(solution)/shard_map/gather_plane/pallas_call | solution.py:171
  174.7 13.6 %attend.2.c_ref = bf16[256,640]{1,0:T(8,128)(2,1)} custom-call(s32[3]{0:T(128)} %pad_add_fusion.meta_ref, bf16[256,640]{1,0:T(8,128)(2,1)} %get-tuple-element.9.q_ref, bf16[8,2,2,128,640]{4,3,2,1,0:T(8,128)(2,1)} %bitcast.77, bf16[8,2,2,128,640]{4,3,2,1,0:T(8,128)(2,1)} %bitcast.78, bf16[8,2,2,128,640]{4,3,2,1,0:T(8,128)(2,1)} %bitcast.79, ...), custom_call_target="tpu_custom_call" | custom-call | flops 2684354560 | bytes 10485760 | tf_op jit(solution)/shard_map/attend/pallas_call | solution.py:233
  188.3 4.8 %output_terms.2 = bf16[4,256,640]{2,1,0:T(8,128)(2,1)} custom-call(bf16[256,640]{1,0:T(8,128)(2,1)} %attend.2.c_ref, bf16[640,2560]{1,0:T(8,128)(2,1)} %w_ref.3), custom_call_target="tpu_custom_call" | custom-call | tf_op jit(solution)/shard_map/output_terms/pallas_call | solution.py:257
  193.1 1.0 slice_bitcast_fusion.1
  194.2 29.2 %reduce-scatter.3.cloned.1.call-done = bf16[1,256,640]{2,1,0:T(8,128)(2,1)} async-done(((bf16[4,256,640]{2,1,0:T(8,128)(2,1)}), bf16[1,256,640]{2,1,0:T(8,128)(2,1)}) %reduce-scatter.3.cloned.1.call-update) | async-done | bytes 327696 | tf_op jit(solution)/shard_map/reduce_scatter | solution.py:319
  223.3 1.0 slice_bitcast_fusion.3
  224.4 1.0 select_select_fusion
  225.3 20.9 %all_to_all.10 = bf16[8,128,640]{2,1,0:T(8,128)(2,1)S(1)} all-to-all(bf16[8,128,640]{2,1,0:T(8,128)(2,1)S(1)} %select_select_fusion), channel_id=1, replica_groups=mesh['dp'=2,'ctx'=4,'tensor'=4] {'dp','ctx'}, dimensions={0} | all-to-all | bytes 2621440 | tf_op jit(solution)/shard_map/all_to_all | solution.py:326
  246.3 9.4 %fusion.5 = bf16[1,4096,640]{2,1,0:T(8,128)(2,1)} fusion(bf16[1024,640]{1,0:T(8,128)(2,1)S(1)} %bitcast.85, s32[4096]{0:T(1024)S(1)} %get-tuple-element.13), kind=kOutput, calls=%fused_computation.7 | convolution fusion | flops 5375524864 | bytes 6569984 | tf_op jit(solution)/shard_map/dot_general | solution.py:328
  (33 shorter events, 5.6 us)
Async XLA Ops:
  33.7 20.8 %all-to-all-start = ((bf16[8,128,640]{2,1,0:T(8,128)(2,1)}), bf16[8,128,640]{2,1,0:T(8,128)(2,1)S(1)}, u32[]{:S(2)}, u32[]{:S(2)}) async-start(bf16[8,128,640]{2,1,0:T(8,128)(2,1)} %bitcast.12), calls=%async_computation | async-start | bytes 2621440 | tf_op jit(solution)/shard_map/all_to_all | solution.py:291
  37.3 52.2 %all-gather.5.cloned.1.call-start = ((), (), s32[]{:S(2)}) async-start(), calls=%async_computation.5 | async-start | bytes 1638400 | tf_op jit(solution)/shard_map/all_gather | solution.py:311
  56.5 82.3 %all-gather.3.cloned.1.call-start = ((), (), s32[]{:S(2)}) async-start(), calls=%async_computation.4 | async-start | bytes 1638400 | tf_op jit(solution)/shard_map/all_gather | solution.py:311
  57.2 135.9 %reduce-scatter.5.cloned.1.call-start = ((), (), s32[]{:S(2)}) async-start(), calls=%async_computation.7 | async-start | bytes 1638400 | tf_op jit(solution)/shard_map/reduce_scatter | solution.py:319
  138.7 84.7 %reduce-scatter.3.cloned.1.call-start = ((), (), s32[]{:S(2)}) async-start(), calls=%async_computation.6 | async-start | bytes 1638400 | tf_op jit(solution)/shard_map/reduce_scatter | solution.py:319
Sparse Core Ops, SparseCore 0:
  56.6 32.7 all-gather.4
  91.0 31.6 all-gather.2
  138.8 30.1 reduce-scatter.4
  193.2 30.0 reduce-scatter.2

commit v3 on v1

--- a/solution.py
+++ b/solution.py
@@ -19,7 +19,7 @@
 PLANE = ("dp", "ctx")
 
 
-def project_kernel(x_ref, w_ref, o_ref, normed):
+def project_kernel(x_ref, w_ref, q_ref, kv_ref, normed):
     part = pl.program_id(0)
     shards, rows, width = x_ref.shape
 
@@ -36,85 +36,145 @@
     acc = jnp.dot(normed[0], w_ref[0, :width], preferred_element_type=jnp.float32)
     for z in range(1, shards):
         acc = acc + jnp.dot(normed[z], w_ref[0, z * width : (z + 1) * width], preferred_element_type=jnp.float32)
-    scale = jnp.where(part == 0, score_scale, 1.0)
-    for h in range(acc.shape[1] // HD):
-        head = acc[:, h * HD : (h + 1) * HD]
-        factor = lax.rsqrt(jnp.mean(head * head, axis=1, keepdims=True) + head_epsilon) * scale
-        factor = jnp.where(part == 2, 1.0, factor)
-        o_ref[0, :, h * HD : (h + 1) * HD] = (head * factor).astype(jnp.bfloat16)
+    heads = acc.shape[1] // HD
+
+    def head_normed(scale):
+        parts = []
+        for h in range(heads):
+            head = acc[:, h * HD : (h + 1) * HD]
+            factor = lax.rsqrt(jnp.mean(head * head, axis=1, keepdims=True) + head_epsilon) * scale
+            parts.append((head * factor).astype(jnp.bfloat16))
+        return parts
+
+    @pl.when(part == 0)
+    def _():
+        for h, value in enumerate(head_normed(score_scale)):
+            q_ref[:, h * HD : (h + 1) * HD] = value
+
+    @pl.when(part == 1)
+    def _():
+        for h, value in enumerate(head_normed(1.0)):
+            kv_ref[0, :, h * HD : (h + 1) * HD] = value
+
+    @pl.when(part == 2)
+    def _():
+        kv_ref[0] = acc.astype(jnp.bfloat16)
 
 
 def project(rows_all, weight):
     shards, rows, width = rows_all.shape
     head_width = weight.shape[2]
+    flops = 2 * rows * shards * width * 3 * head_width
     return pl.pallas_call(
         project_kernel,
         grid=(3,),
-        out_shape=jax.ShapeDtypeStruct((3, rows, head_width), jnp.bfloat16),
+        out_shape=[
+            jax.ShapeDtypeStruct((rows, head_width), jnp.bfloat16),
+            jax.ShapeDtypeStruct((2, rows, head_width), jnp.bfloat16),
+        ],
         in_specs=[
             pl.BlockSpec((shards, rows, width), lambda p: (0, 0, 0)),
             pl.BlockSpec((1, shards * width, head_width), lambda p: (p, 0, 0)),
         ],
-        out_specs=pl.BlockSpec((1, rows, head_width), lambda p: (p, 0, 0)),
+        out_specs=[
+            pl.BlockSpec((rows, head_width), lambda p: (0, 0)),
+            pl.BlockSpec((1, rows, head_width), lambda p: (jnp.maximum(p - 1, 0), 0, 0)),
+        ],
         scratch_shapes=[pltpu.VMEM((shards, rows, width), jnp.bfloat16)],
         compiler_params=pltpu.CompilerParams(vmem_limit_bytes=VMEM_LIMIT),
+        cost_estimate=pl.CostEstimate(flops=flops, bytes_accessed=2 * weight.size, transcendentals=0),
         name="project",
     )(rows_all, weight)
 
 
-def attend_kernel(docs, meta_ref, q_ref, k_ref, v_ref, o_ref):
-    stripe = pl.program_id(1)
-    plane, stripes, size, _ = k_ref.shape
-    period = plane * size
+def gather_plane(kv):
+    docs, ctx_count = lax.axis_size("dp"), lax.axis_size("ctx")
+    if (docs, ctx_count) != (2, 4):
+        return [(lax.all_gather(kv, PLANE, axis=0), jnp.zeros((), jnp.int32))]
+    me = lax.axis_index("dp") * ctx_count + lax.axis_index("ctx")
+    plane = docs * ctx_count
+    x_flip, y_flip, core_flip = ctx_count, 2, 1
+
+    def move(value, flip):
+        return lax.ppermute(value, PLANE, [(i, i ^ flip) for i in range(plane)])
+
+    from_x = move(kv, x_flip)
+    from_y = move(kv, y_flip)
+    even = lax.rem(me, 2) == 0
+    onward = jnp.where(even, from_y, from_x)
+    from_diagonal = lax.ppermute(
+        onward, PLANE, [(i, i ^ (y_flip if i % 2 else x_flip)) for i in range(plane)]
+    )
+    blocks = [(kv, 0), (move(kv, core_flip), core_flip)]
+    for value, flip in ((from_x, x_flip), (from_y, y_flip), (from_diagonal, x_flip ^ y_flip)):
+        blocks.append((value, flip))
+        blocks.append((move(value, core_flip), flip ^ core_flip))
+    return [(value[None], me ^ flip) for value, flip in blocks]
+
+
+def attend_kernel(docs, base, stripes, period, meta_ref, q_ref, *refs):
+    o_ref = refs[-1]
+    rows = q_ref.shape[0]
+    size = rows // stripes
     me = meta_ref[docs]
-    query = q_ref[...]
-    q_index = stripe * period + me * size + lax.broadcasted_iota(jnp.int32, (size, 1), 0)
-    begin = jnp.zeros((size, 1), jnp.int32)
+
+    def index_of(at, place, first):
+        return (first + at // size) * period + place * size + lax.rem(at, size)
+
+    q_index = index_of(lax.broadcasted_iota(jnp.int32, (rows, 1), 0), me, base)
+    lane_at = lax.broadcasted_iota(jnp.int32, (1, rows), 1)
+    begin = jnp.zeros((rows, 1), jnp.int32)
     for d in range(docs):
         begin = jnp.where(q_index >= meta_ref[d], meta_ref[d], begin)
-    lane = lax.broadcasted_iota(jnp.int32, (size, period), 1)
-
-    def tile(at, carry, diagonal):
-        num, den = carry
-        keys = k_ref[:, pl.ds(at, 1)].reshape(period, HD)
-        values = v_ref[:, pl.ds(at, 1)].reshape(period, HD)
-        scores = lax.dot_general(query, keys, (((1,), (1,)), ((), ())), preferred_element_type=jnp.float32)
-        allowed = lane >= begin - at * period
-        if diagonal:
-            allowed = allowed & (lane <= q_index - at * period)
-        weights = jnp.where(allowed, jnp.exp(scores), 0.0)
-        den = den + jnp.sum(weights, axis=1, keepdims=True)
-        num = num + jnp.dot(weights.astype(jnp.bfloat16), values, preferred_element_type=jnp.float32)
-        return num, den
-
-    carry = (jnp.zeros((size, HD), jnp.float32), jnp.zeros((size, 1), jnp.float32))
-    carry = lax.fori_loop(0, stripe, lambda at, c: tile(at, c, False), carry)
-    num, den = tile(stripe, carry, True)
+    query = q_ref[...]
+    num = jnp.zeros((rows, HD), jnp.float32)
+    den = jnp.zeros((rows, 1), jnp.float32)
+    arrays = (len(refs) - 1) // 2
+    per_chunk = arrays // (base // stripes + 1)
+    for i in range(arrays):
+        k_ref, v_ref = refs[2 * i], refs[2 * i + 1]
+        first = i // per_chunk * stripes
+        for piece in range(k_ref.shape[0]):
+            k_index = index_of(lane_at, meta_ref[docs + 1 + i] + piece, first)
+            scores = lax.dot_general(
+                query, k_ref[piece], (((1,), (1,)), ((), ())), preferred_element_type=jnp.float32
+            )
+            allowed = k_index >= begin
+            if first == base:
+                allowed = allowed & (k_index <= q_index)
+            weights = jnp.where(allowed, jnp.exp(scores), 0.0)
+            den = den + jnp.sum(weights, axis=1, keepdims=True)
+            num = num + jnp.dot(weights.astype(jnp.bfloat16), v_ref[piece], preferred_element_type=jnp.float32)
     o_ref[...] = (num / den).astype(jnp.bfloat16)
 
 
-def attend(meta, queries, kv, docs, stripes):
+def attend(meta, queries, kvs, chunk, docs, stripes, period):
     rows, head_width = queries.shape
-    plane = kv.shape[0]
-    size = rows // stripes
     heads = head_width // HD
-    kv = kv.reshape(plane, 2, stripes, size, head_width)
+    operands, specs = [], []
+    for kv, _ in kvs:
+        for which in range(2):
+            operands.append(kv)
+            specs.append(
+                pl.BlockSpec((kv.shape[0], None, rows, HD), lambda h, m, which=which: (0, which, 0, h))
+            )
+    meta = jnp.concatenate([meta, jnp.stack([place for _, place in kvs]).astype(jnp.int32)])
+    pairs = rows * rows * sum(kv.shape[0] for kv, _ in kvs)
     return pl.pallas_call(
-        functools.partial(attend_kernel, docs),
+        functools.partial(attend_kernel, docs, chunk * stripes, stripes, period),
         grid_spec=pltpu.PrefetchScalarGridSpec(
             num_scalar_prefetch=1,
-            grid=(heads, stripes),
-            in_specs=[
-                pl.BlockSpec((size, HD), lambda h, k, m: (k, h)),
-                pl.BlockSpec((plane, None, stripes, size, HD), lambda h, k, m: (0, 0, 0, 0, h)),
-                pl.BlockSpec((plane, None, stripes, size, HD), lambda h, k, m: (0, 1, 0, 0, h)),
-            ],
-            out_specs=pl.BlockSpec((size, HD), lambda h, k, m: (k, h)),
+            grid=(heads,),
+            in_specs=[pl.BlockSpec((rows, HD), lambda h, m: (0, h))] + specs,
+            out_specs=pl.BlockSpec((rows, HD), lambda h, m: (0, h)),
         ),
         out_shape=jax.ShapeDtypeStruct((rows, head_width), jnp.bfloat16),
         compiler_params=pltpu.CompilerParams(vmem_limit_bytes=VMEM_LIMIT),
+        cost_estimate=pl.CostEstimate(
+            flops=4 * pairs * head_width, bytes_accessed=2 * queries.size, transcendentals=pairs * heads
+        ),
         name="attend",
-    )(meta, queries, kv, kv)
+    )(meta, queries, *operands)
 
 
 def output_kernel(c_ref, w_ref, o_ref):
@@ -172,14 +232,22 @@
         packed = jnp.where(owned[b][:, :, None], received[b][None], packed)
     packed = packed.reshape(ACT_DEV, -1)
 
-    rows_all = lax.all_gather(packed, "tensor", axis=0)
+    chunks = 4
+    chunk_stripes = stripes // chunks
+    chunk_rows = ACT_DEV // chunks
     weight = jnp.transpose(qkv_weight, (1, 0, 2))
-    projected = project(rows_all, weight)
-    kv = lax.all_gather(projected[1:], PLANE, axis=0)
     meta = jnp.concatenate([starts[::ctx_count], me[None]]).astype(jnp.int32)
-    context = attend(meta, projected[0], kv, docs, stripes)
-    terms = output_terms(context, out_weight, shards)
-    rows_back = lax.psum_scatter(terms, "tensor", scatter_dimension=0)
+    rows_all = [
+        lax.all_gather(packed[c * chunk_rows : (c + 1) * chunk_rows], "tensor", axis=0) for c in range(chunks)
+    ]
+    kvs, backs = [], []
+    for c in range(chunks):
+        queries, kv = project(rows_all[c], weight)
+        kvs = kvs + gather_plane(kv)
+        context = attend(meta, queries, kvs, c, docs, chunk_stripes, CAP)
+        terms = output_terms(context, out_weight, shards)
+        backs.append(lax.psum_scatter(terms, "tensor", scatter_dimension=0))
+    rows_back = jnp.concatenate(backs, axis=0)
 
     rows_back = rows_back.reshape(stripes, size, -1)
     returned = jnp.where(owned[:, 0][:, :, None], rows_back[0][None], zero)

time: 313 us -> 337 us (1.077)
  waiting for transfers between devices: 184 us -> 65.9 us
  blocking collectives: 30.4 us -> 116 us
  Pallas kernels: 44.4 us -> 83.5 us
  starting transfers between devices: 3.88 us -> 19.4 us
    all_gather x2 -> x0, waiting for transfers between devices: 114 us -> none  [the longest x1 59.3 us: per_device(): kv = lax.all_gather(projected[1:], PLANE, axis=0)]
    all_gather x0 -> x4, blocking collectives: none -> 85.5 us  [per_device(): lax.all_gather(packed[c * chunk_rows:(c + 1) * chunk_rows], 'tensor', axi...]
    reduce_scatter x1 -> x4, waiting for transfers between devices: 52.4 us -> 20.5 us  [per_device(): backs.append(lax.psum_scatter(terms, 'tensor', scatter_dimension=0))]
    ppermute x0 -> x28, waiting for transfers between devices: none -> 28.4 us  [the longest x4 20.7 us: gather_plane(): lax.ppermute(onward, PLANE, [(i, i ^ (y_flip if i % 2 else x_flip)) for i...]
    pallas_call x2 -> x8, Pallas kernels: 38.5 us -> 66 us  [the longest x4 38.6 us: attend(): pl.pallas_call(functools.partial(attend_kernel, docs, chunk * stripes, st...]
    ppermute x0 -> x28, starting transfers between devices: none -> 15.4 us  [the longest x24 11.6 us: move(): return lax.ppermute(value, PLANE, [(i, i ^ flip) for i in range(plane)])]
    pallas_call x1 -> x4, Pallas kernels: 5.9 us -> 17.5 us  [output_terms(): pl.pallas_call(output_kernel, grid=(shards,), out_shape=jax.ShapeDtypeStr...]
    unnamed x3 -> x69, local copies, waits for them, and re-layouts: 2.76 us -> 6.24 us
  transfers between devices with their start and end apart: 4 -> 33, of which waited for: 4 -> 9; matrix products, arithmetic and copies ran while one was open for 1% -> 1% of each run, Pallas kernels for 0% -> 23%
where the time goes in v3:
time: 337 us; the launch traced here: 335 us
  blocking collectives  116 us (34%)
  Pallas kernels  83.5 us (25%)
  waiting for transfers between devices  65.9 us (20%)
  matrix products  20.2 us (6%)
  starting transfers between devices  19.4 us (6%)
  between operations  13.6 us (4%)
  local copies, waits for them, and re-layouts  9.87 us (3%)
  other arithmetic  6.61 us (2%)
    all_gather x4, blocking collectives, per_device(): lax.all_gather(packed[c * chunk_rows:(c + 1) * chunk_rows], 'tensor', axi...  85.5 us
    pallas_call x4, Pallas kernels, attend(): pl.pallas_call(functools.partial(attend_kernel, docs, chunk * stripes, st...  38.6 us
    pallas_call x4, Pallas kernels, project(): pl.pallas_call(project_kernel, grid=(3,), out_shape=[jax.ShapeDtypeStruct...  27.3 us
    all_to_all x1, blocking collectives, per_device(): landed = lax.all_to_all(returned, PLANE, 0, 0).reshape(CAP, -1)  20.9 us
    ppermute x4, waiting for transfers between devices, gather_plane(): lax.ppermute(onward, PLANE, [(i, i ^ (y_flip if i % 2 else x_flip)) for i...  20.7 us
    reduce_scatter x4, waiting for transfers between devices, per_device(): backs.append(lax.psum_scatter(terms, 'tensor', scatter_dimension=0))  20.5 us
    pallas_call x4, Pallas kernels, output_terms(): pl.pallas_call(output_kernel, grid=(shards,), out_shape=jax.ShapeDtypeStr...  17.5 us
    all_to_all x1, waiting for transfers between devices, per_device(): received = lax.all_to_all(dealt.reshape(plane, size, -1), PLANE, 0, 0)  16.9 us
  transfers between devices with their start and end apart: 33, of which 9 were waited for; matrix products, arithmetic and copies ran while one was open for 1% of the time, Pallas kernels for 23%

profile of v3, /device:TPU:0, one launch (start us, length us, event | category | flops | bytes accessed | tf_op | source)
XLA Modules:
  0.0 335.0 jit_solution(18368026014976784764)
XLA Ops:
  10.7 9.5 %all-reduce = s32[8]{0:T(128)S(1)} all-reduce(s32[8]{0:T(128)S(1)} %dynamic-update-slice), channel_id=1, replica_groups=mesh['dp'=2,'ctx'=4,'tensor'=4] {'dp','ctx'}, use_global_device_ids=true, to_apply=%add | all-reduce | flops 8 | bytes 64
  23.0 10.8 %fusion.7 = bf16[1024,640]{1,0:T(8,128)(2,1)} fusion(bf16[1,4096,640]{2,1,0:T(8,128)(2,1)} %param.4, s32[4096]{0:T(1024)S(1)} %bitcast.277), kind=kOutput, calls=%fused_computation.9 | convolution fusion | flops 5373558784 | bytes 6569984 | tf_op jit(solution)/shard_map/dot_general | solution.py:220
  37.7 16.9 %all-to-all-done = bf16[8,128,640]{2,1,0:T(8,128)(2,1)S(1)} async-done(((bf16[8,128,640]{2,1,0:T(8,128)(2,1)}), bf16[8,128,640]{2,1,0:T(8,128)(2,1)S(1)}, u32[]{:S(2)}, u32[]{:S(2)}) %all-to-all-start) | async-done | bytes 1310752 | tf_op jit(solution)/shard_map/all_to_all | solution.py:221
  55.7 17.8 %all_gather.21.x_ref = bf16[4,128,640]{2,1,0:T(8,128)(2,1)} all-gather(bf16[1,128,640]{2,1,0:T(8,128)(2,1)S(1)} %get-tuple-element.34), channel_id=1, replica_groups=mesh['dp'=2,'ctx'=4,'tensor'=4] {'tensor'}, dimensions={0}, use_global_device_ids=true | all-gather | bytes 819200 | tf_op jit(solution)/shard_map/all_gather | solution.py:241
  73.6 6.8 %project.5 = (bf16[128,640]{1,0:T(8,128)(2,1)}, bf16[2,128,640]{2,1,0:T(8,128)(2,1)}) custom-call(bf16[4,128,640]{2,1,0:T(8,128)(2,1)} %all_gather.21.x_ref, bf16[3,2560,640]{2,1,0:T(8,128)(2,1)} %bitcast.106), custom_call_target="tpu_custom_call" | custom-call | flops 1258291200 | bytes 9830400 | tf_op jit(solution)/shard_map/project/pallas_call | solution.py:68
  82.4 5.5 %collective-permute-done.1 = bf16[2,128,640]{2,1,0:T(8,128)(2,1)S(1)} collective-permute-done((bf16[2,128,640]{2,1,0:T(8,128)(2,1)}, bf16[2,128,640]{2,1,0:T(8,128)(2,1)S(1)}, u32[]{:S(2)}, u32[]{:S(2)}) %collective-permute-start.1) | collective-permute-done | bytes 327712 | tf_op jit(solution)/shard_map/ppermute | solution.py:99
  91.7 4.5 %collective-permute-done.5 = bf16[2,128,640]{2,1,0:T(8,128)(2,1)S(1)} collective-permute-done((bf16[2,128,640]{2,1,0:T(8,128)(2,1)S(1)}, bf16[2,128,640]{2,1,0:T(8,128)(2,1)S(1)}, u32[]{:S(2)}, u32[]{:S(2)}) %collective-permute-start.5) | collective-permute-done | bytes 327712 | tf_op jit(solution)/shard_map/ppermute | solution.py:105
  96.3 22.0 %all_gather.22.x_ref = bf16[4,128,640]{2,1,0:T(8,128)(2,1)} all-gather(bf16[1,128,640]{2,1,0:T(8,128)(2,1)S(1)} %get-tuple-element.33), channel_id=1, replica_groups=mesh['dp'=2,'ctx'=4,'tensor'=4] {'tensor'}, dimensions={0}, use_global_device_ids=true | all-gather | bytes 819200 | tf_op jit(solution)/shard_map/all_gather | solution.py:241
  118.3 6.8 %project.6 = (bf16[128,640]{1,0:T(8,128)(2,1)}, bf16[2,128,640]{2,1,0:T(8,128)(2,1)}) custom-call(bf16[4,128,640]{2,1,0:T(8,128)(2,1)} %all_gather.22.x_ref, bf16[3,2560,640]{2,1,0:T(8,128)(2,1)} %bitcast.107), custom_call_target="tpu_custom_call" | custom-call | flops 1258291200 | bytes 9830400 | tf_op jit(solution)/shard_map/project/pallas_call | solution.py:68
  128.6 6.2 %attend.7.c_ref = bf16[128,640]{1,0:T(8,128)(2,1)} custom-call(s32[11]{0:T(128)} %concatenate.21.meta_ref, bf16[128,640]{1,0:T(8,128)(2,1)} %get-tuple-element.20.q_ref, bf16[1,2,128,640]{3,2,1,0:T(8,128)(2,1)} %bitcast.126, bf16[1,2,128,640]{3,2,1,0:T(8,128)(2,1)} %bitcast.127, bf16[1,2,128,640]{3,2,1,0:T(8,128)(2,1)} %bitcast.142, ...), custom_call_target="tpu_custom_call" | custom-call | flops 335544320 | bytes 163840 | tf_op jit(solution)/shard_map/attend/pallas_call | solution.py:163
  141.1 5.3 %collective-permute-done.12 = bf16[2,128,640]{2,1,0:T(8,128)(2,1)S(1)} collective-permute-done((bf16[2,128,640]{2,1,0:T(8,128)(2,1)S(1)}, bf16[2,128,640]{2,1,0:T(8,128)(2,1)S(1)}, u32[]{:S(2)}, u32[]{:S(2)}) %collective-permute-start.12) | collective-permute-done | bytes 327712 | tf_op jit(solution)/shard_map/ppermute | solution.py:105
  146.5 23.4 %all_gather.23.x_ref = bf16[4,128,640]{2,1,0:T(8,128)(2,1)} all-gather(bf16[1,128,640]{2,1,0:T(8,128)(2,1)S(1)} %get-tuple-element.32), channel_id=1, replica_groups=mesh['dp'=2,'ctx'=4,'tensor'=4] {'tensor'}, dimensions={0}, use_global_device_ids=true | all-gather | bytes 819200 | tf_op jit(solution)/shard_map/all_gather | solution.py:241
  169.9 6.8 %project.7 = (bf16[128,640]{1,0:T(8,128)(2,1)}, bf16[2,128,640]{2,1,0:T(8,128)(2,1)}) custom-call(bf16[4,128,640]{2,1,0:T(8,128)(2,1)} %all_gather.23.x_ref, bf16[3,2560,640]{2,1,0:T(8,128)(2,1)} %bitcast.108), custom_call_target="tpu_custom_call" | custom-call | flops 1258291200 | bytes 9830400 | tf_op jit(solution)/shard_map/project/pallas_call | solution.py:68
  180.2 8.2 %attend.6.c_ref = bf16[128,640]{1,0:T(8,128)(2,1)} custom-call(s32[19]{0:T(128)} %concatenate.20.meta_ref, bf16[128,640]{1,0:T(8,128)(2,1)} %get-tuple-element.19.q_ref, bf16[1,2,128,640]{3,2,1,0:T(8,128)(2,1)} %bitcast.128, bf16[1,2,128,640]{3,2,1,0:T(8,128)(2,1)} %bitcast.129, bf16[1,2,128,640]{3,2,1,0:T(8,128)(2,1)} %bitcast.144, ...), custom_call_target="tpu_custom_call" | custom-call | flops 671088640 | bytes 163840 | tf_op jit(solution)/shard_map/attend/pallas_call | solution.py:163
  188.3 4.4 %output_terms.6 = bf16[4,128,640]{2,1,0:T(8,128)(2,1)} custom-call(bf16[128,640]{1,0:T(8,128)(2,1)} %attend.6.c_ref, bf16[640,2560]{1,0:T(8,128)(2,1)} %w_ref.7), custom_call_target="tpu_custom_call" | custom-call | tf_op jit(solution)/shard_map/output_terms/pallas_call | solution.py:187
  195.0 5.1 %collective-permute-done.19 = bf16[2,128,640]{2,1,0:T(8,128)(2,1)S(1)} collective-permute-done((bf16[2,128,640]{2,1,0:T(8,128)(2,1)S(1)}, bf16[2,128,640]{2,1,0:T(8,128)(2,1)S(1)}, u32[]{:S(2)}, u32[]{:S(2)}) %collective-permute-start.19) | collective-permute-done | bytes 327712 | tf_op jit(solution)/shard_map/ppermute | solution.py:105
  200.1 22.3 %all_gather.20.x_ref = bf16[4,128,640]{2,1,0:T(8,128)(2,1)} all-gather(bf16[1,128,640]{2,1,0:T(8,128)(2,1)S(1)} %get-tuple-element.31), channel_id=1, replica_groups=mesh['dp'=2,'ctx'=4,'tensor'=4] {'tensor'}, dimensions={0}, use_global_device_ids=true | all-gather | bytes 819200 | tf_op jit(solution)/shard_map/all_gather | solution.py:241
  222.4 6.8 %project.4 = (bf16[128,640]{1,0:T(8,128)(2,1)}, bf16[2,128,640]{2,1,0:T(8,128)(2,1)}) custom-call(bf16[4,128,640]{2,1,0:T(8,128)(2,1)} %all_gather.20.x_ref, bf16[3,2560,640]{2,1,0:T(8,128)(2,1)} %bitcast.109), custom_call_target="tpu_custom_call" | custom-call | flops 1258291200 | bytes 9830400 | tf_op jit(solution)/shard_map/project/pallas_call | solution.py:68
  232.7 10.8 %attend.5.c_ref = bf16[128,640]{1,0:T(8,128)(2,1)} custom-call(s32[27]{0:T(128)} %concatenate.19.meta_ref, bf16[128,640]{1,0:T(8,128)(2,1)} %get-tuple-element.18.q_ref, bf16[1,2,128,640]{3,2,1,0:T(8,128)(2,1)} %bitcast.130, bf16[1,2,128,640]{3,2,1,0:T(8,128)(2,1)} %bitcast.131, bf16[1,2,128,640]{3,2,1,0:T(8,128)(2,1)} %bitcast.146, ...), custom_call_target="tpu_custom_call" | custom-call | flops 1006632960 | bytes 163840 | tf_op jit(solution)/shard_map/attend/pallas_call | solution.py:163
  249.7 5.7 %collective-permute-done.26 = bf16[2,128,640]{2,1,0:T(8,128)(2,1)S(1)} collective-permute-done((bf16[2,128,640]{2,1,0:T(8,128)(2,1)S(1)}, bf16[2,128,640]{2,1,0:T(8,128)(2,1)S(1)}, u32[]{:S(2)}, u32[]{:S(2)}) %collective-permute-start.26) | collective-permute-done | bytes 327712 | tf_op jit(solution)/shard_map/ppermute | solution.py:105
  257.8 13.5 %attend.4.c_ref = bf16[128,640]{1,0:T(8,128)(2,1)} custom-call(s32[35]{0:T(128)} %concatenate.18.meta_ref, bf16[128,640]{1,0:T(8,128)(2,1)} %get-tuple-element.13.q_ref, bf16[1,2,128,640]{3,2,1,0:T(8,128)(2,1)} %bitcast.132, bf16[1,2,128,640]{3,2,1,0:T(8,128)(2,1)} %bitcast.133, bf16[1,2,128,640]{3,2,1,0:T(8,128)(2,1)} %bitcast.148, ...), custom_call_target="tpu_custom_call" | custom-call | flops 1342177280 | bytes 163840 | tf_op jit(solution)/shard_map/attend/pallas_call | solution.py:163
  275.8 20.5 %reduce-scatter.5.cloned.1.call-done = bf16[1,128,640]{2,1,0:T(8,128)(2,1)} async-done(((bf16[4,128,640]{2,1,0:T(8,128)(2,1)}), bf16[1,128,640]{2,1,0:T(8,128)(2,1)}) %reduce-scatter.5.cloned.1.call-update) | async-done | bytes 163856 | tf_op jit(solution)/shard_map/reduce_scatter | solution.py:249
  298.2 20.9 %all_to_all.10 = bf16[8,128,640]{2,1,0:T(8,128)(2,1)S(1)} all-to-all(bf16[8,128,640]{2,1,0:T(8,128)(2,1)S(1)} %select_select_fusion), channel_id=1, replica_groups=mesh['dp'=2,'ctx'=4,'tensor'=4] {'dp','ctx'}, dimensions={0} | all-to-all | bytes 2621440 | tf_op jit(solution)/shard_map/all_to_all | solution.py:256
  319.1 9.4 %fusion.5 = bf16[1,4096,640]{2,1,0:T(8,128)(2,1)} fusion(bf16[1024,640]{1,0:T(8,128)(2,1)S(1)} %bitcast.258, s32[4096]{0:T(1024)S(1)} %get-tuple-element.21), kind=kOutput, calls=%fused_computation.7 | convolution fusion | flops 5375524864 | bytes 6569984 | tf_op jit(solution)/shard_map/dot_general | solution.py:258
  (164 shorter events, 51.3 us)
Async XLA Ops:
  33.8 20.8 %all-to-all-start = ((bf16[8,128,640]{2,1,0:T(8,128)(2,1)}), bf16[8,128,640]{2,1,0:T(8,128)(2,1)S(1)}, u32[]{:S(2)}, u32[]{:S(2)}) async-start(bf16[8,128,640]{2,1,0:T(8,128)(2,1)} %bitcast.19), calls=%async_computation | async-start | bytes 2621440 | tf_op jit(solution)/shard_map/all_to_all | solution.py:221
  37.4 238.4 %reduce-scatter.11.cloned.1.call-start = ((), (), s32[]{:S(2)}) async-start(), calls=%async_computation.9 | async-start | bytes 819200 | tf_op jit(solution)/shard_map/reduce_scatter | solution.py:249
  81.0 8.1 %collective-permute-start.3 = (bf16[2,128,640]{2,1,0:T(8,128)(2,1)}, bf16[2,128,640]{2,1,0:T(8,128)(2,1)S(1)}, u32[]{:S(2)}, u32[]{:S(2)}) collective-permute-start(bf16[2,128,640]{2,1,0:T(8,128)(2,1)} %get-tuple-element.14), channel_id=1, source_target_pairs={{0,8},{4,12},{8,0},{12,4},{16,24},{20,28},{24,16},{28,20},{1,9},{5... | collective-permute-start | bytes 983048 | tf_op jit(solution)/shard_map/ppermute | solution.py:99
  91.2 35.0 %collective-permute-start = (bf16[2,128,640]{2,1,0:T(8,128)(2,1)}, bf16[2,128,640]{2,1,0:T(8,128)(2,1)S(1)}, u32[]{:S(2)}, u32[]{:S(2)}) collective-permute-start(bf16[2,128,640]{2,1,0:T(8,128)(2,1)} %get-tuple-element.14), channel_id=1, source_target_pairs={{0,4},{4,0},{8,12},{12,8},{16,20},{20,16},{24,28},{28,24},{1,5},{5... | collective-permute-start | bytes 983048 | tf_op jit(solution)/shard_map/ppermute | solution.py:99
  91.2 36.4 %collective-permute-start.2 = (bf16[2,128,640]{2,1,0:T(8,128)(2,1)S(1)}, bf16[2,128,640]{2,1,0:T(8,128)(2,1)S(1)}, u32[]{:S(2)}, u32[]{:S(2)}) collective-permute-start(bf16[2,128,640]{2,1,0:T(8,128)(2,1)S(1)} %collective-permute-done.1), channel_id=1, source_target_pairs={{0,4},{4,0},{8,12},{12,8},{16,20},{20,16},{24,28},{28,24},{1,5},{5... | collective-permute-start | bytes 983048 | tf_op jit(solution)/shard_map/ppermute | solution.py:99
  91.7 35.9 %collective-permute-start.4 = (bf16[2,128,640]{2,1,0:T(8,128)(2,1)S(1)}, bf16[2,128,640]{2,1,0:T(8,128)(2,1)S(1)}, u32[]{:S(2)}, u32[]{:S(2)}) collective-permute-start(bf16[2,128,640]{2,1,0:T(8,128)(2,1)S(1)} %collective-permute-done.3), channel_id=1, source_target_pairs={{0,4},{4,0},{8,12},{12,8},{16,20},{20,16},{24,28},{28,24},{1,5},{5... | collective-permute-start | bytes 983048 | tf_op jit(solution)/shard_map/ppermute | solution.py:99
  96.3 31.3 %collective-permute-start.6 = (bf16[2,128,640]{2,1,0:T(8,128)(2,1)S(1)}, bf16[2,128,640]{2,1,0:T(8,128)(2,1)S(1)}, u32[]{:S(2)}, u32[]{:S(2)}) collective-permute-start(bf16[2,128,640]{2,1,0:T(8,128)(2,1)S(1)} %collective-permute-done.5), channel_id=1, source_target_pairs={{0,4},{4,0},{8,12},{12,8},{16,20},{20,16},{24,28},{28,24},{1,5},{5... | collective-permute-start | bytes 983048 | tf_op jit(solution)/shard_map/ppermute | solution.py:99
  125.1 14.1 %collective-permute-start.8 = (bf16[2,128,640]{2,1,0:T(8,128)(2,1)}, bf16[2,128,640]{2,1,0:T(8,128)(2,1)S(1)}, u32[]{:S(2)}, u32[]{:S(2)}) collective-permute-start(bf16[2,128,640]{2,1,0:T(8,128)(2,1)} %get-tuple-element.15), channel_id=1, source_target_pairs={{0,16},{4,20},{8,24},{12,28},{16,0},{20,4},{24,8},{28,12},{1,17},{... | collective-permute-start | bytes 983048 | tf_op jit(solution)/shard_map/ppermute | solution.py:99
  126.2 13.0 %collective-permute-start.10 = (bf16[2,128,640]{2,1,0:T(8,128)(2,1)}, bf16[2,128,640]{2,1,0:T(8,128)(2,1)S(1)}, u32[]{:S(2)}, u32[]{:S(2)}) collective-permute-start(bf16[2,128,640]{2,1,0:T(8,128)(2,1)} %get-tuple-element.15), channel_id=1, source_target_pairs={{0,8},{4,12},{8,0},{12,4},{16,24},{20,28},{24,16},{28,20},{1,9},{5... | collective-permute-start | bytes 983048 | tf_op jit(solution)/shard_map/ppermute | solution.py:99
  139.2 136.6 %reduce-scatter.9.cloned.1.call-start = ((), (), s32[]{:S(2)}) async-start(), calls=%async_computation.8 | async-start | bytes 819200 | tf_op jit(solution)/shard_map/reduce_scatter | solution.py:249
  140.6 37.4 %collective-permute-start.7 = (bf16[2,128,640]{2,1,0:T(8,128)(2,1)S(1)}, bf16[2,128,640]{2,1,0:T(8,128)(2,1)S(1)}, u32[]{:S(2)}, u32[]{:S(2)}) collective-permute-start(bf16[2,128,640]{2,1,0:T(8,128)(2,1)S(1)} %copy-done.9), channel_id=1, source_target_pairs={{0,4},{4,0},{8,12},{12,8},{16,20},{20,16},{24,28},{28,24},{1,5},{5... | collective-permute-start | bytes 983048 | tf_op jit(solution)/shard_map/ppermute | solution.py:99
  140.6 38.6 %collective-permute-start.9 = (bf16[2,128,640]{2,1,0:T(8,128)(2,1)S(1)}, bf16[2,128,640]{2,1,0:T(8,128)(2,1)S(1)}, u32[]{:S(2)}, u32[]{:S(2)}) collective-permute-start(bf16[2,128,640]{2,1,0:T(8,128)(2,1)S(1)} %collective-permute-done.8), channel_id=1, source_target_pairs={{0,4},{4,0},{8,12},{12,8},{16,20},{20,16},{24,28},{28,24},{1,5},{5... | collective-permute-start | bytes 983048 | tf_op jit(solution)/shard_map/ppermute | solution.py:99
  141.1 38.1 %collective-permute-start.11 = (bf16[2,128,640]{2,1,0:T(8,128)(2,1)S(1)}, bf16[2,128,640]{2,1,0:T(8,128)(2,1)S(1)}, u32[]{:S(2)}, u32[]{:S(2)}) collective-permute-start(bf16[2,128,640]{2,1,0:T(8,128)(2,1)S(1)} %collective-permute-done.10), channel_id=1, source_target_pairs={{0,4},{4,0},{8,12},{12,8},{16,20},{20,16},{24,28},{28,24},{1,5},{5... | collective-permute-start | bytes 983048 | tf_op jit(solution)/shard_map/ppermute | solution.py:99
  146.4 32.8 %collective-permute-start.13 = (bf16[2,128,640]{2,1,0:T(8,128)(2,1)S(1)}, bf16[2,128,640]{2,1,0:T(8,128)(2,1)S(1)}, u32[]{:S(2)}, u32[]{:S(2)}) collective-permute-start(bf16[2,128,640]{2,1,0:T(8,128)(2,1)S(1)} %collective-permute-done.12), channel_id=1, source_target_pairs={{0,4},{4,0},{8,12},{12,8},{16,20},{20,16},{24,28},{28,24},{1,5},{5... | collective-permute-start | bytes 983048 | tf_op jit(solution)/shard_map/ppermute | solution.py:99
  176.7 16.1 %collective-permute-start.15 = (bf16[2,128,640]{2,1,0:T(8,128)(2,1)}, bf16[2,128,640]{2,1,0:T(8,128)(2,1)S(1)}, u32[]{:S(2)}, u32[]{:S(2)}) collective-permute-start(bf16[2,128,640]{2,1,0:T(8,128)(2,1)} %get-tuple-element.16), channel_id=1, source_target_pairs={{0,16},{4,20},{8,24},{12,28},{16,0},{20,4},{24,8},{28,12},{1,17},{... | collective-permute-start | bytes 983048 | tf_op jit(solution)/shard_map/ppermute | solution.py:99
  178.0 14.8 %collective-permute-start.17 = (bf16[2,128,640]{2,1,0:T(8,128)(2,1)}, bf16[2,128,640]{2,1,0:T(8,128)(2,1)S(1)}, u32[]{:S(2)}, u32[]{:S(2)}) collective-permute-start(bf16[2,128,640]{2,1,0:T(8,128)(2,1)} %get-tuple-element.16), channel_id=1, source_target_pairs={{0,8},{4,12},{8,0},{12,4},{16,24},{20,28},{24,16},{28,20},{1,9},{5... | collective-permute-start | bytes 983048 | tf_op jit(solution)/shard_map/ppermute | solution.py:99
  192.8 83.0 %reduce-scatter.7.cloned.1.call-start = ((), (), s32[]{:S(2)}) async-start(), calls=%async_computation.7 | async-start | bytes 819200 | tf_op jit(solution)/shard_map/reduce_scatter | solution.py:249
  194.5 36.1 %collective-permute-start.14 = (bf16[2,128,640]{2,1,0:T(8,128)(2,1)S(1)}, bf16[2,128,640]{2,1,0:T(8,128)(2,1)S(1)}, u32[]{:S(2)}, u32[]{:S(2)}) collective-permute-start(bf16[2,128,640]{2,1,0:T(8,128)(2,1)S(1)} %copy-done.17), channel_id=1, source_target_pairs={{0,4},{4,0},{8,12},{12,8},{16,20},{20,16},{24,28},{28,24},{1,5},{5... | collective-permute-start | bytes 983048 | tf_op jit(solution)/shard_map/ppermute | solution.py:99
  194.5 37.3 %collective-permute-start.16 = (bf16[2,128,640]{2,1,0:T(8,128)(2,1)S(1)}, bf16[2,128,640]{2,1,0:T(8,128)(2,1)S(1)}, u32[]{:S(2)}, u32[]{:S(2)}) collective-permute-start(bf16[2,128,640]{2,1,0:T(8,128)(2,1)S(1)} %collective-permute-done.15), channel_id=1, source_target_pairs={{0,4},{4,0},{8,12},{12,8},{16,20},{20,16},{24,28},{28,24},{1,5},{5... | collective-permute-start | bytes 983048 | tf_op jit(solution)/shard_map/ppermute | solution.py:99
  195.0 36.8 %collective-permute-start.18 = (bf16[2,128,640]{2,1,0:T(8,128)(2,1)S(1)}, bf16[2,128,640]{2,1,0:T(8,128)(2,1)S(1)}, u32[]{:S(2)}, u32[]{:S(2)}) collective-permute-start(bf16[2,128,640]{2,1,0:T(8,128)(2,1)S(1)} %collective-permute-done.17), channel_id=1, source_target_pairs={{0,4},{4,0},{8,12},{12,8},{16,20},{20,16},{24,28},{28,24},{1,5},{5... | collective-permute-start | bytes 983048 | tf_op jit(solution)/shard_map/ppermute | solution.py:99
  200.1 31.7 %collective-permute-start.20 = (bf16[2,128,640]{2,1,0:T(8,128)(2,1)S(1)}, bf16[2,128,640]{2,1,0:T(8,128)(2,1)S(1)}, u32[]{:S(2)}, u32[]{:S(2)}) collective-permute-start(bf16[2,128,640]{2,1,0:T(8,128)(2,1)S(1)} %collective-permute-done.19), channel_id=1, source_target_pairs={{0,4},{4,0},{8,12},{12,8},{16,20},{20,16},{24,28},{28,24},{1,5},{5... | collective-permute-start | bytes 983048 | tf_op jit(solution)/shard_map/ppermute | solution.py:99
  229.2 19.0 %collective-permute-start.22 = (bf16[2,128,640]{2,1,0:T(8,128)(2,1)}, bf16[2,128,640]{2,1,0:T(8,128)(2,1)S(1)}, u32[]{:S(2)}, u32[]{:S(2)}) collective-permute-start(bf16[2,128,640]{2,1,0:T(8,128)(2,1)} %get-tuple-element.17), channel_id=1, source_target_pairs={{0,16},{4,20},{8,24},{12,28},{16,0},{20,4},{24,8},{28,12},{1,17},{... | collective-permute-start | bytes 983048 | tf_op jit(solution)/shard_map/ppermute | solution.py:99
  230.6 17.6 %collective-permute-start.24 = (bf16[2,128,640]{2,1,0:T(8,128)(2,1)}, bf16[2,128,640]{2,1,0:T(8,128)(2,1)S(1)}, u32[]{:S(2)}, u32[]{:S(2)}) collective-permute-start(bf16[2,128,640]{2,1,0:T(8,128)(2,1)} %get-tuple-element.17), channel_id=1, source_target_pairs={{0,8},{4,12},{8,0},{12,4},{16,24},{20,28},{24,16},{28,20},{1,9},{5... | collective-permute-start | bytes 983048 | tf_op jit(solution)/shard_map/ppermute | solution.py:99
  247.9 48.3 %reduce-scatter.5.cloned.1.call-start = ((), (), s32[]{:S(2)}) async-start(), calls=%async_computation.6 | async-start | bytes 819200 | tf_op jit(solution)/shard_map/reduce_scatter | solution.py:249
  (40 other events, 419.2 us)
Sparse Core Ops, SparseCore 0:
  139.3 26.1 reduce-scatter.10
  192.9 24.3 reduce-scatter.8
  248.1 20.4 reduce-scatter.6
  275.8 20.4 reduce-scatter.4

commit v4 on v2

--- a/solution.py
+++ b/solution.py
@@ -17,6 +17,66 @@
 head_epsilon = 1e-06
 VMEM_LIMIT = 60 * 1024 * 1024
 PLANE = ("dp", "ctx")
+
+
+def exchange_kernel(plane, x_ref, o_ref, send_sem, recv_sem, local_sem):
+    ctx_count = lax.axis_size("ctx")
+    me = lax.axis_index("dp") * ctx_count + lax.axis_index("ctx")
+
+    def device(place):
+        return {"dp": place // ctx_count, "ctx": lax.rem(place, ctx_count)}
+
+    barrier = pltpu.get_barrier_semaphore()
+    for step in range(1, plane):
+        target = device(lax.rem(me + step, plane))
+        pl.semaphore_signal(barrier, inc=1, device_id=target, device_id_type=pl.DeviceIdType.MESH)
+    pl.semaphore_wait(barrier, plane - 1)
+
+    sends = []
+    for step in range(1, plane):
+        place = lax.rem(me + step, plane)
+        copy = pltpu.make_async_remote_copy(
+            src_ref=x_ref.at[place],
+            dst_ref=o_ref.at[me],
+            send_sem=send_sem.at[step],
+            recv_sem=recv_sem.at[step],
+            device_id=device(place),
+            device_id_type=pl.DeviceIdType.MESH,
+        )
+        copy.start()
+        sends.append(copy)
+    local = pltpu.make_async_copy(x_ref.at[me], o_ref.at[me], local_sem)
+    local.start()
+    for step in range(1, plane):
+        origin = lax.rem(me + plane - step, plane)
+        pltpu.make_async_remote_copy(
+            src_ref=x_ref.at[origin],
+            dst_ref=o_ref.at[origin],
+            send_sem=send_sem.at[step],
+            recv_sem=recv_sem.at[step],
+            device_id=device(origin),
+            device_id_type=pl.DeviceIdType.MESH,
+        ).wait_recv()
+    for copy in sends:
+        copy.wait_send()
+    local.wait()
+
+
+def exchange(x, call):
+    plane = x.shape[0]
+    return pl.pallas_call(
+        functools.partial(exchange_kernel, plane),
+        out_shape=jax.ShapeDtypeStruct(x.shape, x.dtype),
+        in_specs=[pl.BlockSpec(memory_space=pltpu.VMEM)],
+        out_specs=pl.BlockSpec(memory_space=pltpu.VMEM),
+        scratch_shapes=[
+            pltpu.SemaphoreType.DMA((plane,)),
+            pltpu.SemaphoreType.DMA((plane,)),
+            pltpu.SemaphoreType.DMA,
+        ],
+        compiler_params=pltpu.CompilerParams(collective_id=call, has_side_effects=True),
+        name="exchange",
+    )(x)
 
 
 def project_kernel(x_ref, w_ref, q_ref, kv_ref, normed):
@@ -281,14 +341,14 @@
 
     active = depth[0] >= RECURSION
     ones = active.astype(jnp.int32)
-    counts = lax.all_gather(jnp.sum(ones)[None], PLANE, axis=0, tiled=True)
+    counts = exchange(jnp.broadcast_to(jnp.sum(ones), (plane, 8, HD)), 2)[:, 0, 0]
     ends = jnp.cumsum(counts)
     starts = ends - counts
     rank = jnp.cumsum(ones) - 1
     slot = jnp.where(active, lax.rem(starts[me] + rank, CAP), -1)
     onehot = (jnp.arange(CAP, dtype=jnp.int32)[:, None] == slot[None, :]).astype(jnp.bfloat16)
     dealt = jnp.dot(onehot, tokens, preferred_element_type=jnp.float32).astype(jnp.bfloat16)
-    received = lax.all_to_all(dealt.reshape(plane, size, -1), PLANE, 0, 0)
+    received = exchange(dealt.reshape(plane, size, -1), 3)
 
     index = (
         jnp.arange(stripes, dtype=jnp.int32)[:, None] * CAP
@@ -323,7 +383,7 @@
     returned = jnp.where(owned[:, 0][:, :, None], rows_back[0][None], zero)
     for k in range(1, stripes):
         returned = jnp.where(owned[:, k][:, :, None], rows_back[k][None], returned)
-    landed = lax.all_to_all(returned, PLANE, 0, 0).reshape(CAP, -1)
+    landed = exchange(returned, 4).reshape(CAP, -1)
     spread = (slot[:, None] == jnp.arange(CAP, dtype=jnp.int32)[None, :]).astype(jnp.bfloat16)
     update = jnp.dot(spread, landed, preferred_element_type=jnp.float32).astype(jnp.bfloat16)
     return update[None]

time: 263 us -> 265 us (level)
  Pallas kernels: 104 us -> 150 us
  blocking collectives: 30.4 us -> 0 us
  waiting for transfers between devices: 78.1 us -> 62.5 us
  starting transfers between devices: 3.91 us -> 0.3 us
    pallas_call x0 -> x3, Pallas kernels: none -> 46.6 us  [exchange(): pl.pallas_call(functools.partial(exchange_kernel, plane), out_shape=jax.S...]
    all_to_all x1 -> x0, blocking collectives: 20.9 us -> none  [per_device(): landed = lax.all_to_all(returned, PLANE, 0, 0).reshape(CAP, -1)]
    all_to_all x1 -> x0, waiting for transfers between devices: 16.9 us -> none  [per_device(): received = lax.all_to_all(dealt.reshape(plane, size, -1), PLANE, 0, 0)]
    unnamed x1 -> x0, blocking collectives: 9.49 us -> none
    all_to_all x1 -> x0, starting transfers between devices: 3.57 us -> none  [per_device(): received = lax.all_to_all(dealt.reshape(plane, size, -1), PLANE, 0, 0)]
    unnamed x7 -> x4, local copies, waits for them, and re-layouts: 2.68 us -> 0.03 us
  transfers between devices with their start and end apart: 5 -> 4, of which waited for: 3 -> 2; matrix products, arithmetic and copies ran while one was open for 1% -> 1% of each run, Pallas kernels for 39% -> 39%
where the time goes in v4:
time: 265 us; the launch traced here: 264 us
  Pallas kernels  150 us (57%)
  waiting for transfers between devices  62.5 us (24%)
  matrix products  21.5 us (8%)
  between operations  13.3 us (5%)
  other arithmetic  8.04 us (3%)
  local copies, waits for them, and re-layouts  7.76 us (3%)
    pallas_call x2, Pallas kernels, gather_plane(): pl.pallas_call(functools.partial(gather_kernel, pieces), out_shape=jax.Sh...  54.3 us
    pallas_call x3, Pallas kernels, exchange(): pl.pallas_call(functools.partial(exchange_kernel, plane), out_shape=jax.S...  46.6 us
    all_gather x2, waiting for transfers between devices, per_device(): lax.all_gather(packed[c * chunk_rows:(c + 1) * chunk_rows], 'tensor', axi...  32.6 us
    reduce_scatter x2, waiting for transfers between devices, per_device(): backs.append(lax.psum_scatter(terms, 'tensor', scatter_dimension=0))  29.2 us
    pallas_call x2, Pallas kernels, attend(): pl.pallas_call(functools.partial(attend_kernel, docs, (len(kvs) - 1) * st...  22.5 us
    pallas_call x2, Pallas kernels, project(): pl.pallas_call(project_kernel, grid=(3,), out_shape=[jax.ShapeDtypeStruct...  17.2 us
    dot_general x1, matrix products, per_device(): jnp.dot(onehot, tokens, preferred_element_type=jnp.float32)  10.8 us
    dot_general x1, matrix products, per_device(): jnp.dot(spread, landed, preferred_element_type=jnp.float32)  10.7 us
  transfers between devices with their start and end apart: 4, of which 2 were waited for; matrix products, arithmetic and copies ran while one was open for 1% of the time, Pallas kernels for 39%

profile of v4, /device:TPU:0, one launch (start us, length us, event | category | flops | bytes accessed | tf_op | source)
XLA Modules:
  0.0 263.5 jit_solution(2717824145680658733)
XLA Ops:
  8.6 1.3 broadcast_in_dim.213.x_ref
  10.0 7.7 %exchange.3 = s32[8,8,128]{2,1,0:T(8,128)} custom-call(s32[8,8,128]{2,1,0:T(8,128)} %broadcast_in_dim.213.x_ref), custom_call_target="tpu_custom_call" | custom-call | tf_op jit(solution)/shard_map/exchange/pallas_call | solution.py:67
  17.6 1.0 slice_reduce_fusion.1
  18.9 1.0 subtract_reduce_fusion
  22.1 10.8 %fusion.7 = bf16[1024,640]{1,0:T(8,128)(2,1)} fusion(bf16[1,4096,640]{2,1,0:T(8,128)(2,1)} %param.4, s32[4096]{0:T(1024)S(1)} %bitcast.88), kind=kOutput, calls=%fused_computation.9 | convolution fusion | flops 5373558784 | bytes 6569984 | tf_op jit(solution)/shard_map/dot_general | solution.py:350
  32.9 19.5 %exchange.4 = bf16[8,128,640]{2,1,0:T(8,128)(2,1)} custom-call(bf16[8,128,640]{2,1,0:T(8,128)(2,1)} %bitcast.85), custom_call_target="tpu_custom_call" | custom-call | tf_op jit(solution)/shard_map/exchange/pallas_call | solution.py:67
  52.3 1.5 slice_bitcast_fusion.11
  53.9 1.0 select_select_fusion.1
  54.9 0.9 fusion.16
  57.5 32.6 %all-gather.5.cloned.1.call-done.x_ref = bf16[4,256,640]{2,1,0:T(8,128)(2,1)} async-done(((bf16[1,256,640]{2,1,0:T(8,128)(2,1)}), bf16[4,256,640]{2,1,0:T(8,128)(2,1)}) %all-gather.5.cloned.1.call-update) | async-done | bytes 1310736 | tf_op jit(solution)/shard_map/all_gather | solution.py:371
  90.1 8.5 %project.3 = (bf16[256,640]{1,0:T(8,128)(2,1)}, bf16[2,256,640]{2,1,0:T(8,128)(2,1)}) custom-call(bf16[4,256,640]{2,1,0:T(8,128)(2,1)} %all-gather.5.cloned.1.call-done.x_ref, bf16[3,2560,640]{2,1,0:T(8,128)(2,1)} %bitcast.80), custom_call_target="tpu_custom_call" | custom-call | flops 2516582400 | bytes 9830400 | tf_op jit(solution)/shard_map/project/pallas_call | solution.py:128
  98.7 27.0 %gather_plane.2 = bf16[8,2,256,640]{3,2,1,0:T(8,128)(2,1)} custom-call(bf16[2,256,640]{2,1,0:T(8,128)(2,1)} %get-tuple-element.10.kv_ref), custom_call_target="tpu_custom_call" | custom-call | bytes 60000000 | tf_op jit(solution)/shard_map/gather_plane/pallas_call | solution.py:231
  125.7 8.9 %attend.3.c_ref = bf16[256,640]{1,0:T(8,128)(2,1)} custom-call(s32[3]{0:T(128)} %pad_add_fusion.meta_ref, bf16[256,640]{1,0:T(8,128)(2,1)} %get-tuple-element.12.q_ref, bf16[8,2,2,128,640]{4,3,2,1,0:T(8,128)(2,1)} %bitcast.74, bf16[8,2,2,128,640]{4,3,2,1,0:T(8,128)(2,1)} %bitcast.75), custom_call_target="tpu_custom_call" | custom-call | flops 1342177280 | bytes 10485760 | tf_op jit(solution)/shard_map/attend/pallas_call | solution.py:293
  134.6 4.8 %output_terms.3 = bf16[4,256,640]{2,1,0:T(8,128)(2,1)} custom-call(bf16[256,640]{1,0:T(8,128)(2,1)} %attend.3.c_ref, bf16[640,2560]{1,0:T(8,128)(2,1)} %w_ref.3), custom_call_target="tpu_custom_call" | custom-call | tf_op jit(solution)/shard_map/output_terms/pallas_call | solution.py:317
  139.5 8.7 %project.2 = (bf16[256,640]{1,0:T(8,128)(2,1)}, bf16[2,256,640]{2,1,0:T(8,128)(2,1)}) custom-call(bf16[4,256,640]{2,1,0:T(8,128)(2,1)} %all-gather.3.cloned.1.call-done.x_ref, bf16[3,2560,640]{2,1,0:T(8,128)(2,1)} %bitcast.81), custom_call_target="tpu_custom_call" | custom-call | flops 2516582400 | bytes 9830400 | tf_op jit(solution)/shard_map/project/pallas_call | solution.py:128
  148.1 27.3 %gather_plane.3 = bf16[8,2,256,640]{3,2,1,0:T(8,128)(2,1)} custom-call(bf16[2,256,640]{2,1,0:T(8,128)(2,1)} %get-tuple-element.11.kv_ref), custom_call_target="tpu_custom_call" | custom-call | bytes 60000000 | tf_op jit(solution)/shard_map/gather_plane/pallas_call | solution.py:231
  175.4 13.6 %attend.2.c_ref = bf16[256,640]{1,0:T(8,128)(2,1)} custom-call(s32[3]{0:T(128)} %pad_add_fusion.meta_ref, bf16[256,640]{1,0:T(8,128)(2,1)} %get-tuple-element.9.q_ref, bf16[8,2,2,128,640]{4,3,2,1,0:T(8,128)(2,1)} %bitcast.76, bf16[8,2,2,128,640]{4,3,2,1,0:T(8,128)(2,1)} %bitcast.77, bf16[8,2,2,128,640]{4,3,2,1,0:T(8,128)(2,1)} %bitcast.78, ...), custom_call_target="tpu_custom_call" | custom-call | flops 2684354560 | bytes 10485760 | tf_op jit(solution)/shard_map/attend/pallas_call | solution.py:293
  189.0 4.8 %output_terms.2 = bf16[4,256,640]{2,1,0:T(8,128)(2,1)} custom-call(bf16[256,640]{1,0:T(8,128)(2,1)} %attend.2.c_ref, bf16[640,2560]{1,0:T(8,128)(2,1)} %w_ref.3), custom_call_target="tpu_custom_call" | custom-call | tf_op jit(solution)/shard_map/output_terms/pallas_call | solution.py:317
  193.9 1.0 slice_bitcast_fusion.1
  194.9 29.2 %reduce-scatter.3.cloned.1.call-done = bf16[1,256,640]{2,1,0:T(8,128)(2,1)} async-done(((bf16[4,256,640]{2,1,0:T(8,128)(2,1)}), bf16[1,256,640]{2,1,0:T(8,128)(2,1)}) %reduce-scatter.3.cloned.1.call-update) | async-done | bytes 327696 | tf_op jit(solution)/shard_map/reduce_scatter | solution.py:379
  224.0 1.0 slice_bitcast_fusion.3
  225.1 1.8 select_select_fusion.x_ref
  226.8 19.5 %exchange.5 = bf16[8,128,640]{2,1,0:T(8,128)(2,1)} custom-call(bf16[8,128,640]{2,1,0:T(8,128)(2,1)} %select_select_fusion.x_ref), custom_call_target="tpu_custom_call" | custom-call | tf_op jit(solution)/shard_map/exchange/pallas_call | solution.py:67
  246.3 10.7 %fusion.5 = bf16[1,4096,640]{2,1,0:T(8,128)(2,1)} fusion(bf16[1024,640]{1,0:T(8,128)(2,1)} %bitcast.84, s32[4096]{0:T(1024)S(1)} %get-tuple-element.13), kind=kOutput, calls=%fused_computation.7 | convolution fusion | flops 5375524864 | bytes 6569984 | tf_op jit(solution)/shard_map/dot_general | solution.py:388
  (33 shorter events, 6.4 us)
Async XLA Ops:
  6.5 83.6 %all-gather.5.cloned.1.call-start = ((), (), s32[]{:S(2)}) async-start(), calls=%async_computation.3 | async-start | bytes 1638400 | tf_op jit(solution)/shard_map/all_gather | solution.py:371
  55.8 83.7 %all-gather.3.cloned.1.call-start = ((), (), s32[]{:S(2)}) async-start(), calls=%async_computation.2 | async-start | bytes 1638400 | tf_op jit(solution)/shard_map/all_gather | solution.py:371
  56.5 137.3 %reduce-scatter.5.cloned.1.call-start = ((), (), s32[]{:S(2)}) async-start(), calls=%async_computation.5 | async-start | bytes 1638400 | tf_op jit(solution)/shard_map/reduce_scatter | solution.py:379
  139.4 84.7 %reduce-scatter.3.cloned.1.call-start = ((), (), s32[]{:S(2)}) async-start(), calls=%async_computation.4 | async-start | bytes 1638400 | tf_op jit(solution)/shard_map/reduce_scatter | solution.py:379
Sparse Core Ops, SparseCore 0:
  55.9 34.1 all-gather.4
  91.7 31.6 all-gather.2
  139.5 30.1 reduce-scatter.4
  193.9 30.0 reduce-scatter.2

commit v5 on v2

--- a/solution.py
+++ b/solution.py
@@ -166,7 +166,7 @@
     docs, ctx_count = lax.axis_size("dp"), lax.axis_size("ctx")
     if (docs, ctx_count) != (2, 4):
         return lax.all_gather(kv, PLANE, axis=0)
-    pieces = 4
+    pieces = 8
     plane = docs * ctx_count
     return pl.pallas_call(
         functools.partial(gather_kernel, pieces),
@@ -185,8 +185,9 @@
 
 
 def attend_kernel(docs, base, meta_ref, q_ref, *refs):
-    o_ref = refs[-1]
-    pairs = [(refs[i], refs[i + 1]) for i in range(0, len(refs) - 1, 2)]
+    w_ref, o_ref, total = refs[-3:]
+    pairs = [(refs[i], refs[i + 1]) for i in range(0, len(refs) - 3, 2)]
+    head = pl.program_id(0)
     plane, stripes, size, _ = refs[0].shape
     period = plane * size
     rows = stripes * size
@@ -213,10 +214,25 @@
             den = den + jnp.sum(weights, axis=1, keepdims=True)
             num = num + jnp.dot(weights.astype(jnp.bfloat16), values, preferred_element_type=jnp.float32)
             at += 1
-    o_ref[...] = (num / den).astype(jnp.bfloat16)
-
-
-def attend(meta, queries, kvs, docs, stripes):
+    context = (num / den).astype(jnp.bfloat16)
+    term = jnp.dot(context, w_ref[...], preferred_element_type=jnp.float32)
+
+    @pl.when(head == 0)
+    def _():
+        total[...] = term
+
+    @pl.when(head > 0)
+    def _():
+        total[...] += term
+
+    @pl.when(head == pl.num_programs(0) - 1)
+    def _():
+        width = o_ref.shape[2]
+        for z in range(o_ref.shape[0]):
+            o_ref[z] = total[:, z * width : (z + 1) * width].astype(jnp.bfloat16)
+
+
+def attend(meta, queries, kvs, out_weight, shards, docs, stripes):
     rows, head_width = queries.shape
     plane = kvs[0].shape[0]
     size = rows // stripes
@@ -229,6 +245,9 @@
             specs.append(
                 pl.BlockSpec((plane, None, stripes, size, HD), lambda h, m, which=which: (0, which, 0, 0, h))
             )
+    width = out_weight.shape[1]
+    operands.append(out_weight)
+    specs.append(pl.BlockSpec((HD, width), lambda h, m: (h, 0)))
     pairs = rows * plane * rows * len(kvs)
     return pl.pallas_call(
         functools.partial(attend_kernel, docs, (len(kvs) - 1) * stripes),
@@ -236,36 +255,16 @@
             num_scalar_prefetch=1,
             grid=(heads,),
             in_specs=[pl.BlockSpec((rows, HD), lambda h, m: (0, h))] + specs,
-            out_specs=pl.BlockSpec((rows, HD), lambda h, m: (0, h)),
+            out_specs=pl.BlockSpec((shards, rows, width // shards), lambda h, m: (0, 0, 0)),
+            scratch_shapes=[pltpu.VMEM((rows, width), jnp.float32)],
         ),
-        out_shape=jax.ShapeDtypeStruct((rows, head_width), jnp.bfloat16),
+        out_shape=jax.ShapeDtypeStruct((shards, rows, width // shards), jnp.bfloat16),
         compiler_params=pltpu.CompilerParams(vmem_limit_bytes=VMEM_LIMIT),
         cost_estimate=pl.CostEstimate(
             flops=4 * pairs * head_width, bytes_accessed=4 * kvs[0].size, transcendentals=pairs * heads
         ),
         name="attend",
     )(meta, queries, *operands)
-
-
-def output_kernel(c_ref, w_ref, o_ref):
-    o_ref[0] = jnp.dot(c_ref[...], w_ref[...], preferred_element_type=jnp.float32).astype(jnp.bfloat16)
-
-
-def output_terms(context, out_weight, shards):
-    rows, head_width = context.shape
-    width = out_weight.shape[1] // shards
-    return pl.pallas_call(
-        output_kernel,
-        grid=(shards,),
-        out_shape=jax.ShapeDtypeStruct((shards, rows, width), jnp.bfloat16),
-        in_specs=[
-            pl.BlockSpec((rows, head_width), lambda z: (0, 0)),
-            pl.BlockSpec((head_width, width), lambda z: (0, z)),
-        ],
-        out_specs=pl.BlockSpec((1, rows, width), lambda z: (z, 0, 0)),
-        compiler_params=pltpu.CompilerParams(vmem_limit_bytes=VMEM_LIMIT),
-        name="output_terms",
-    )(context, out_weight)
 
 
 def per_device(hidden, depth, qkv_weight, out_weight):
@@ -314,8 +313,7 @@
     for c in range(chunks):
         queries, kv = project(rows_all[c], weight)
         kvs.append(gather_plane(kv, c))
-        context = attend(meta, queries, kvs, docs, chunk_stripes)
-        terms = output_terms(context, out_weight, shards)
+        terms = attend(meta, queries, kvs, out_weight, shards, docs, chunk_stripes)
         backs.append(lax.psum_scatter(terms, "tensor", scatter_dimension=0))
     rows_back = jnp.concatenate(backs, axis=0)
 

time: 263 us -> 262 us (level)
    pallas_call x2 -> x0, Pallas kernels: 9.61 us -> none  [output_terms(): pl.pallas_call(output_kernel, grid=(shards,), out_shape=jax.ShapeDtypeStr...]
    pallas_call x2, Pallas kernels: 22.5 us -> 30.4 us  [attend(): pl.pallas_call(functools.partial(attend_kernel, docs, (len(kvs) - 1) * st...]
where the time goes in v5:
time: 262 us; the launch traced here: 261 us
  Pallas kernels  103 us (39%)
  waiting for transfers between devices  78.1 us (30%)
  blocking collectives  30.4 us (12%)
  matrix products  20.2 us (8%)
  between operations  13.3 us (5%)
  local copies, waits for them, and re-layouts  6.63 us (3%)
  other arithmetic  6.09 us (2%)
  starting transfers between devices  3.91 us (1%)
    pallas_call x2, Pallas kernels, gather_plane(): pl.pallas_call(functools.partial(gather_kernel, pieces), out_shape=jax.Sh...  55.1 us
    all_gather x2, waiting for transfers between devices, per_device(): lax.all_gather(packed[c * chunk_rows:(c + 1) * chunk_rows], 'tensor', axi...  31.3 us
    pallas_call x2, Pallas kernels, attend(): pl.pallas_call(functools.partial(attend_kernel, docs, (len(kvs) - 1) * st...  30.4 us
    reduce_scatter x2, waiting for transfers between devices, per_device(): backs.append(lax.psum_scatter(terms, 'tensor', scatter_dimension=0))  29.2 us
    all_to_all x1, blocking collectives, per_device(): landed = lax.all_to_all(returned, PLANE, 0, 0).reshape(CAP, -1)  20.9 us
    pallas_call x2, Pallas kernels, project(): pl.pallas_call(project_kernel, grid=(3,), out_shape=[jax.ShapeDtypeStruct...  17.2 us
    all_to_all x1, waiting for transfers between devices, per_device(): received = lax.all_to_all(dealt.reshape(plane, size, -1), PLANE, 0, 0)  16.9 us
    dot_general x1, matrix products, per_device(): jnp.dot(onehot, tokens, preferred_element_type=jnp.float32)  10.8 us
  transfers between devices with their start and end apart: 5, of which 3 were waited for; matrix products, arithmetic and copies ran while one was open for 1% of the time, Pallas kernels for 39%

profile of v5, /device:TPU:0, one launch (start us, length us, event | category | flops | bytes accessed | tf_op | source)
XLA Modules:
  0.0 261.3 jit_solution(12537284861384939891)
XLA Ops:
  6.5 0.8 fusion.14
  8.0 1.3 dynamic-slice
  9.2 1.4 dynamic-update-slice
  10.6 9.5 %all-reduce = s32[8]{0:T(128)S(1)} all-reduce(s32[8]{0:T(128)S(1)} %dynamic-update-slice), channel_id=1, replica_groups=mesh['dp'=2,'ctx'=4,'tensor'=4] {'dp','ctx'}, use_global_device_ids=true, to_apply=%add | all-reduce | flops 8 | bytes 64
  21.4 0.7 fusion.11
  22.1 0.8 fusion.13
  22.9 10.8 %fusion.7 = bf16[1024,640]{1,0:T(8,128)(2,1)} fusion(bf16[1,4096,640]{2,1,0:T(8,128)(2,1)} %param.4, s32[4096]{0:T(1024)S(1)} %bitcast.88), kind=kOutput, calls=%fused_computation.9 | convolution fusion | flops 5373558784 | bytes 6569984 | tf_op jit(solution)/shard_map/dot_general | solution.py:289
  33.7 3.6 %all-to-all-start = ((bf16[8,128,640]{2,1,0:T(8,128)(2,1)}), bf16[8,128,640]{2,1,0:T(8,128)(2,1)S(1)}, u32[]{:S(2)}, u32[]{:S(2)}) async-start(bf16[8,128,640]{2,1,0:T(8,128)(2,1)} %bitcast.12), calls=%async_computation | async-start | bytes 2621440 | tf_op jit(solution)/shard_map/all_to_all | solution.py:290
  37.6 16.9 %all-to-all-done = bf16[8,128,640]{2,1,0:T(8,128)(2,1)S(1)} async-done(((bf16[8,128,640]{2,1,0:T(8,128)(2,1)}), bf16[8,128,640]{2,1,0:T(8,128)(2,1)S(1)}, u32[]{:S(2)}, u32[]{:S(2)}) %all-to-all-start) | async-done | bytes 1310752 | tf_op jit(solution)/shard_map/all_to_all | solution.py:290
  54.6 1.0 select_select_fusion.1
  55.6 0.9 fusion.16
  58.1 31.3 %all-gather.5.cloned.1.call-done.x_ref = bf16[4,256,640]{2,1,0:T(8,128)(2,1)} async-done(((bf16[1,256,640]{2,1,0:T(8,128)(2,1)}), bf16[4,256,640]{2,1,0:T(8,128)(2,1)}) %all-gather.5.cloned.1.call-update) | async-done | bytes 1310736 | tf_op jit(solution)/shard_map/all_gather | solution.py:310
  89.4 8.5 %project.3 = (bf16[256,640]{1,0:T(8,128)(2,1)}, bf16[2,256,640]{2,1,0:T(8,128)(2,1)}) custom-call(bf16[4,256,640]{2,1,0:T(8,128)(2,1)} %all-gather.5.cloned.1.call-done.x_ref, bf16[3,2560,640]{2,1,0:T(8,128)(2,1)} %bitcast.81), custom_call_target="tpu_custom_call" | custom-call | flops 2516582400 | bytes 9830400 | tf_op jit(solution)/shard_map/project/pallas_call | solution.py:68
  97.9 27.4 %gather_plane.2 = bf16[8,2,256,640]{3,2,1,0:T(8,128)(2,1)} custom-call(bf16[2,256,640]{2,1,0:T(8,128)(2,1)} %get-tuple-element.10.kv_ref), custom_call_target="tpu_custom_call" | custom-call | bytes 60000000 | tf_op jit(solution)/shard_map/gather_plane/pallas_call | solution.py:171
  125.4 13.1 %attend.3 = bf16[4,256,640]{2,1,0:T(8,128)(2,1)} custom-call(s32[3]{0:T(128)} %pad_add_fusion.meta_ref, bf16[256,640]{1,0:T(8,128)(2,1)} %get-tuple-element.12.q_ref, bf16[8,2,2,128,640]{4,3,2,1,0:T(8,128)(2,1)} %bitcast.75, bf16[8,2,2,128,640]{4,3,2,1,0:T(8,128)(2,1)} %bitcast.76, bf16[640,2560]{1,0:T(8,128)(2,1)} %refs_2_.1), custom_call_target="tpu_custom_call" | custom-call | flops 1342177280 | bytes 10485760 | tf_op jit(solution)/shard_map/attend/pallas_call | solution.py:252
  138.6 8.7 %project.2 = (bf16[256,640]{1,0:T(8,128)(2,1)}, bf16[2,256,640]{2,1,0:T(8,128)(2,1)}) custom-call(bf16[4,256,640]{2,1,0:T(8,128)(2,1)} %all-gather.3.cloned.1.call-done.x_ref, bf16[3,2560,640]{2,1,0:T(8,128)(2,1)} %bitcast.82), custom_call_target="tpu_custom_call" | custom-call | flops 2516582400 | bytes 9830400 | tf_op jit(solution)/shard_map/project/pallas_call | solution.py:68
  147.3 27.7 %gather_plane.3 = bf16[8,2,256,640]{3,2,1,0:T(8,128)(2,1)} custom-call(bf16[2,256,640]{2,1,0:T(8,128)(2,1)} %get-tuple-element.11.kv_ref), custom_call_target="tpu_custom_call" | custom-call | bytes 60000000 | tf_op jit(solution)/shard_map/gather_plane/pallas_call | solution.py:171
  175.0 17.2 %attend.2 = bf16[4,256,640]{2,1,0:T(8,128)(2,1)} custom-call(s32[3]{0:T(128)} %pad_add_fusion.meta_ref, bf16[256,640]{1,0:T(8,128)(2,1)} %get-tuple-element.9.q_ref, bf16[8,2,2,128,640]{4,3,2,1,0:T(8,128)(2,1)} %bitcast.77, bf16[8,2,2,128,640]{4,3,2,1,0:T(8,128)(2,1)} %bitcast.78, bf16[8,2,2,128,640]{4,3,2,1,0:T(8,128)(2,1)} %bitcast.79, ...), custom_call_target="tpu_custom_call" | custom-call | flops 2684354560 | bytes 10485760 | tf_op jit(solution)/shard_map/attend/pallas_call | solution.py:252
  192.3 1.0 slice_bitcast_fusion.1
  193.3 29.1 %reduce-scatter.3.cloned.1.call-done = bf16[1,256,640]{2,1,0:T(8,128)(2,1)} async-done(((bf16[4,256,640]{2,1,0:T(8,128)(2,1)}), bf16[1,256,640]{2,1,0:T(8,128)(2,1)}) %reduce-scatter.3.cloned.1.call-update) | async-done | bytes 327696 | tf_op jit(solution)/shard_map/reduce_scatter | solution.py:317
  222.5 1.0 slice_bitcast_fusion.3
  223.5 1.0 select_select_fusion
  224.5 20.9 %all_to_all.10 = bf16[8,128,640]{2,1,0:T(8,128)(2,1)S(1)} all-to-all(bf16[8,128,640]{2,1,0:T(8,128)(2,1)S(1)} %select_select_fusion), channel_id=1, replica_groups=mesh['dp'=2,'ctx'=4,'tensor'=4] {'dp','ctx'}, dimensions={0} | all-to-all | bytes 2621440 | tf_op jit(solution)/shard_map/all_to_all | solution.py:324
  245.4 9.4 %fusion.5 = bf16[1,4096,640]{2,1,0:T(8,128)(2,1)} fusion(bf16[1024,640]{1,0:T(8,128)(2,1)S(1)} %bitcast.85, s32[4096]{0:T(1024)S(1)} %get-tuple-element.13), kind=kOutput, calls=%fused_computation.7 | convolution fusion | flops 5375524864 | bytes 6569984 | tf_op jit(solution)/shard_map/dot_general | solution.py:326
  (31 shorter events, 4.1 us)
Async XLA Ops:
  33.7 20.8 %all-to-all-start = ((bf16[8,128,640]{2,1,0:T(8,128)(2,1)}), bf16[8,128,640]{2,1,0:T(8,128)(2,1)S(1)}, u32[]{:S(2)}, u32[]{:S(2)}) async-start(bf16[8,128,640]{2,1,0:T(8,128)(2,1)} %bitcast.12), calls=%async_computation | async-start | bytes 2621440 | tf_op jit(solution)/shard_map/all_to_all | solution.py:290
  37.3 52.2 %all-gather.5.cloned.1.call-start = ((), (), s32[]{:S(2)}) async-start(), calls=%async_computation.5 | async-start | bytes 1638400 | tf_op jit(solution)/shard_map/all_gather | solution.py:310
  56.5 82.1 %all-gather.3.cloned.1.call-start = ((), (), s32[]{:S(2)}) async-start(), calls=%async_computation.4 | async-start | bytes 1638400 | tf_op jit(solution)/shard_map/all_gather | solution.py:310
  57.2 135.1 %reduce-scatter.5.cloned.1.call-start = ((), (), s32[]{:S(2)}) async-start(), calls=%async_computation.7 | async-start | bytes 1638400 | tf_op jit(solution)/shard_map/reduce_scatter | solution.py:317
  138.5 83.9 %reduce-scatter.3.cloned.1.call-start = ((), (), s32[]{:S(2)}) async-start(), calls=%async_computation.6 | async-start | bytes 1638400 | tf_op jit(solution)/shard_map/reduce_scatter | solution.py:317
Sparse Core Ops, SparseCore 0:
  56.6 32.7 all-gather.4
  91.0 31.6 all-gather.2
  138.7 30.1 reduce-scatter.4
  192.4 30.0 reduce-scatter.2
